TPU v7x, 32 devices: a whole 2x2x4 slice. The times are simulated.
32 devices in a mesh: row: 8 (over z, y), col: 4 (over x, core).
Axes of the slice: x: 2, y: 2, z: 4, core: 2. Of those that a mesh axis runs over, the one named last changes fastest.
Arguments:
- trailing: float32 [16384, 16384], P('row', 'col'), may hold values from -40 to 40, as said below
- factor_one: float32 [16384, 512], P(('row', 'col')), may hold values from -0.0390625 to 0.0390625
- inverse_one: float32 [512, 512], replicated, may hold values from -1 to 2, as said below
- factor_two_top: float32 [512, 512], replicated, may hold values from -0.0390625 to 0.0390625
- factor_two: float32 [16384, 512], P(('row', 'col')), may hold values from -0.0390625 to 0.0390625
- inverse_two: float32 [512, 512], replicated, may hold values from -1 to 2, as said below
- structure_one: int32 [96], replicated, may hold values from 0 to 127, as said below
- structure_two: int32 [94], replicated, may hold values from 0 to 127, as said below
Outputs:
- column_one: float32 [16384, 512], P(('row', 'col'))
- diagonal_one: float32 [512, 512], replicated
- column_two: float32 [16384, 512], P(('row', 'col'))
- cross_two: float32 [512, 512], replicated
- diagonal_two: float32 [512, 512], replicated
Inputs may be any that keep to these rules, and one draw needn't show every extreme that they name: `trailing`: symmetric. `inverse_one`: lower triangular, diagonal between 1 and 2. `inverse_two`: lower triangular, diagonal between 1 and 2. `structure_one`: distinct, rising; lists block 0 and the last block. `structure_two`: distinct, rising, each also listed in structure_one; lists block 0 and the last block.
All inputs are finite; a program needn't handle non-finite values.
Results may differ from a plain program's by a relative error of at most 0.0003.
Values sent between devices are 32-bit elements; how exact they have to be, the bound alone decides.
A program may use at most 128 MiB of HBM per device.

v0:
```python
import functools

import jax
import jax.numpy as jnp
from jax import lax
from jax.experimental import pallas as pl
from jax.experimental.pallas import tpu as pltpu
from jax.sharding import PartitionSpec as P

BLK = 128
MESH = pl.DeviceIdType.MESH
CH = 8
LAG = 2
RS0 = 9
A0 = 23
F32 = jnp.float32
BF16 = jnp.bfloat16


def product(left, right):
    return jnp.dot(left, right, precision=lax.Precision.HIGHEST, preferred_element_type=jnp.float32)


def big_product(left, right):
    return jnp.dot(left, right, precision=lax.Precision.HIGH, preferred_element_type=jnp.float32)


def block_flags(structure, first_row, count):
    blocks = (first_row + jnp.arange(count, dtype=jnp.int32)) // BLK
    hits = jnp.any(blocks[:, None] == structure[None, :], axis=1)
    return hits.astype(jnp.float32)[:, None]


def split(value):
    high = value.astype(BF16)
    return high, (value - high.astype(F32)).astype(BF16)


def mm(left, right):
    return jnp.dot(left, right, preferred_element_type=F32)


def flip(c, t):
    return ((c // 2 + t // 2) % 2) * 2 + (c % 2 + t % 2) % 2


def panels_kernel(
    trail, n1_in, n2_in, y1_out, y2_out,
    n1buf, n2buf, n2h, n2l, out1, out2, rsu, rsd, rsy, y2buf, tbuf, n1h, n1l, cbuf, xbuf,
    ag_sem, n2_sem, up_sem, dn_sem, ry_sem, y2_sem, t_sem, c_sem, x_sem,
    s_up, s_dn, s_y, s_root, s_n2, s_ry, s_line, s_c, s_x,
):
    r, c = lax.axis_index("row"), lax.axis_index("col")
    z, y, x, k = r // 2, r % 2, c // 2, c % 2
    piece = n1_in.shape[0]
    cr = piece // CH
    wr = n2_in.shape[0] // CH
    ypart = (r + 1 - 2 * y, c)
    cpart = (r, flip(c, 1))
    xpart = (r, flip(c, 2))
    above = (lax.rem(r + 2, 8), c)
    below = (lax.rem(r + 6, 8), c)
    dist = jnp.where(z > c, z - c, c - z)

    def remote(src, dst, send, recv, to):
        return pltpu.make_async_remote_copy(
            src_ref=src, dst_ref=dst, send_sem=send, recv_sem=recv, device_id=to, device_id_type=MESH
        )

    def arrived(ref, sem):
        pltpu.make_async_copy(ref, ref, sem).wait()

    bar = pltpu.get_barrier_semaphore()
    for to in (ypart, cpart, xpart, (r, flip(c, 3))):
        pl.semaphore_signal(bar, inc=1, device_id=to, device_id_type=MESH)

    @pl.when(z < 3)
    def _():
        pl.semaphore_signal(bar, inc=1, device_id=above, device_id_type=MESH)

    @pl.when(z > 0)
    def _():
        pl.semaphore_signal(bar, inc=1, device_id=below, device_id_type=MESH)

    def tile_of(u):
        isa = u // 16
        v = u % 16
        p = v % 8
        tb = (4 - (p + 1) // 2) % 4
        ob = p % 2 + (7 - p) // 7 - p // 7
        hb = (x + v // 8) % 2
        ta, oa, ha = v // 4, (v // 2) % 2, v % 2
        t = isa * ta + (1 - isa) * tb
        o = isa * oa + (1 - isa) * ob
        h = isa * ha + (1 - isa) * hb
        return ((y + o) % 2) * 4 + flip(c, t), h, t, o

    half = 2 * piece

    def fetch(u):
        j, h, _, _ = tile_of(u)
        rows = pl.ds(pl.multiple_of(h * half, half), half)
        cols = pl.ds(pl.multiple_of(j * piece, piece), piece)
        return pltpu.make_async_copy(trail.at[rows, cols], tbuf.at[u % 2], t_sem.at[u % 2])

    fetch(0).start()
    own = pltpu.make_async_copy(n2_in, n2buf.at[c], n2_sem.at[0])
    own.start()

    pl.semaphore_wait(bar, 4 + (z + 2) // 3 + (5 - z) // 3)

    to_x = remote(n2_in, n2buf.at[c], s_n2.at[0], n2_sem.at[2], xpart)
    to_x.start()
    to_c = remote(n2_in, n2buf.at[c], s_n2.at[1], n2_sem.at[1], cpart)
    to_c.start()

    here = y * 4 + c
    for ch in range(CH):
        part = pl.ds(ch * cr, cr)

        @pl.when(c == z)
        def _():
            pltpu.make_async_copy(n1_in.at[part], n1buf.at[here, part], ag_sem.at[here, ch]).start()

        @pl.when(c != z)
        def _():
            remote(n1_in.at[part], n1buf.at[here, part], s_root.at[ch], ag_sem.at[here, ch], (r, z)).start()

    own.wait()
    arrived(n2buf.at[flip(c, 1)], n2_sem.at[1])
    for t in range(2):
        q = flip(c, t)
        n2h[q], n2l[q] = split(n2buf[q])

    def ag_step(n):
        s, ch = n // CH, n % CH
        o = (s + 3) // 4 - (s + 2) // 4
        t = s - (s + 3) // 4
        j = ((y + o) % 2) * 4 + flip(c, t)
        part = pl.ds(pl.multiple_of(ch * cr, cr), cr)
        chunk = n1buf.at[j, part]
        arrived(chunk, ag_sem.at[j, ch])

        @pl.when((z >= c) & (z < 3))
        def _():
            remote(chunk, chunk, s_up.at[n], ag_sem.at[j, ch], above).start()

        @pl.when((z <= c) & (z > 0))
        def _():
            remote(chunk, chunk, s_dn.at[n], ag_sem.at[j, ch], below).start()

        @pl.when((s >= 2) | ((s == 0) & (z == c)))
        def _():
            remote(chunk, chunk, s_y.at[t, ch], ag_sem.at[j, ch], ypart).start()

    def rs_step(n):
        s, ch = n // CH, n % CH
        mine = (s + 3) // 4
        t = (4 - s) * mine
        j = ((y + 1 - mine) % 2) * 4 + flip(c, t)
        part = pl.ds(pl.multiple_of(ch * wr, wr), wr)
        chunk = out2.at[j, part]

        @pl.when((z >= c) & (z < 3))
        def _():
            arrived(rsu.at[s, part], up_sem.at[n])
            chunk[...] += rsu[s, part]

        @pl.when((z <= c) & (z > 0))
        def _():
            arrived(rsd.at[s, part], dn_sem.at[n])
            chunk[...] += rsd[s, part]

        @pl.when(((s >= 1) & (s <= 3)) | ((s == 4) & (z == c)))
        def _():
            arrived(rsy.at[t, part], ry_sem.at[t, ch])
            chunk[...] += rsy[t, part]

        @pl.when(z > c)
        def _():
            remote(chunk, rsu.at[s, part], s_line.at[n], up_sem.at[n], below).start()

        @pl.when(z < c)
        def _():
            remote(chunk, rsd.at[s, part], s_line.at[n], dn_sem.at[n], above).start()

        @pl.when((z == c) & (s == 0))
        def _():
            remote(chunk, rsy.at[0, part], s_line.at[n], ry_sem.at[0, ch], ypart).start()

        @pl.when((z == c) & (s >= 1) & (s <= 3))
        def _():
            remote(chunk, y2buf.at[part], s_line.at[n], y2_sem.at[ch], (r, flip(c, t))).start()

        @pl.when((z == c) & (s == 4))
        def _():
            pltpu.make_async_copy(chunk, y2buf.at[part], y2_sem.at[ch]).start()

    def turn_b(u):
        j, h, t, o = tile_of(u)
        fetch(u).wait()
        fetch(u + 1).start()

        @pl.loop(0, 2)
        def _(i):
            rows = pl.ds(pl.multiple_of(i * piece, piece), piece)
            th, tl = split(tbuf[u % 2, rows])
            q = 2 * h + i
            add = mm(n2h[q], th) + (mm(n2l[q], th) + mm(n2h[q], tl))

            @pl.when((u < 8) & (i == 0))
            def _():
                out2[j] = add

            @pl.when((u >= 8) | (i == 1))
            def _():
                out2[j] += add

        @pl.when((u >= 8) & (o == 1) & (t >= 1))
        def _():
            for ch in range(CH):
                part = pl.ds(ch * wr, wr)
                remote(out2.at[j, part], rsy.at[t, part], s_ry.at[t, ch], ry_sem.at[t, ch], ypart).start()

    def turn_a(u):
        j, h, t, o = tile_of(u)

        @pl.when((h == 0) & (o == 1) & (t >= 1))
        def _():
            for ch in range(CH):
                arrived(n1buf.at[j, pl.ds(ch * cr, cr)], ag_sem.at[j, ch])

        @pl.when(h == 0)
        def _():
            n1h[...], n1l[...] = split(n1buf[j])

        fetch(u).wait()

        @pl.when(u < 31)
        def _():
            fetch(u + 1).start()

        @pl.loop(0, 2)
        def _(i):
            rows = pl.ds(pl.multiple_of(i * piece, piece), piece)
            th, tl = split(tbuf[u % 2, rows])
            add = mm(th, n1h[...]) + (mm(th, n1l[...]) + mm(tl, n1h[...]))
            q = 2 * h + i

            @pl.when(u < 18)
            def _():
                out1[q] = add

            @pl.when(u >= 18)
            def _():
                out1[q] += add

    qx = flip(c, 2)
    end_a = A0 + 28
    ag_first = LAG * dist
    rs_first = RS0 + LAG * jnp.where(z > c, 3 - z, jnp.where(z < c, z, jnp.where(c < 2, 3 - c, c)))

    def core_copy(i):
        to = flip(c, 1 + 2 * (1 - i))
        return remote(out1.at[to], cbuf.at[i], s_c.at[i], c_sem.at[i], cpart)

    x_copy = remote(out1.at[qx], xbuf, s_x.at[0], x_sem.at[0], xpart)

    def tick(step, carry):
        n = step - ag_first

        @pl.when((n >= 0) & (n < 5 * CH))
        def _():
            ag_step(n)

        m = step - rs_first

        @pl.when((m >= 0) & (m < 5 * CH))
        def _():
            rs_step(m)

        @pl.when(step == 8)
        def _():
            got = flip(c, 2)
            arrived(n2buf.at[got], n2_sem.at[2])
            fwd = remote(n2buf.at[got], n2buf.at[got], s_n2.at[2], n2_sem.at[3], cpart)
            fwd.start()
            n2h[got], n2l[got] = split(n2buf[got])
            last = flip(c, 3)
            arrived(n2buf.at[last], n2_sem.at[3])
            n2h[last], n2l[last] = split(n2buf[last])

        @pl.when(step < 16)
        def _():
            turn_b(step)

        w = step - A0

        @pl.when((w >= 0) & (w < 32) & (w % 8 < 4))
        def _():
            turn_a(16 + (w // 8) * 4 + w % 4)

        @pl.when(step == end_a)
        def _():
            core_copy(0).start()
            core_copy(1).start()

        @pl.when(step == end_a + 1)
        def _():
            core_copy(0).wait_recv()
            out1[qx] += cbuf[0]
            x_copy.start()
            core_copy(1).wait_recv()
            out1[c] += cbuf[1]

        return carry

    last_tick = RS0 + 3 * LAG + 5 * CH
    lax.fori_loop(0, max(last_tick, end_a + 2), tick, 0)

    x_copy.wait_recv()
    y1_out[...] = out1[c] + xbuf[...]
    for ch in range(CH):
        part = pl.ds(ch * wr, wr)
        arrived(y2buf.at[part], y2_sem.at[ch])
    y2_out[...] = y2buf[...]

    def sent(ref, sem):
        pltpu.make_async_copy(ref, ref, sem).wait()

    whole = n2buf.at[0]
    for i in range(3):
        sent(whole, s_n2.at[i])
    for i in range(2):
        sent(cbuf.at[0], s_c.at[i])
    sent(xbuf, s_x.at[0])
    bit = n1buf.at[0, pl.ds(0, cr)]
    wbit = out2.at[0, pl.ds(0, wr)]

    @pl.loop(0, 5 * CH)
    def _(n):
        s, ch = n // CH, n % CH

        @pl.when((z >= c) & (z < 3))
        def _():
            sent(bit, s_up.at[n])

        @pl.when((z <= c) & (z > 0))
        def _():
            sent(bit, s_dn.at[n])

        @pl.when((s >= 2) | ((s == 0) & (z == c)))
        def _():
            sent(bit, s_y.at[s - (s + 3) // 4, ch])

        @pl.when((z != c) | (s < 4))
        def _():
            sent(wbit, s_line.at[n])

        @pl.when((s >= 1) & (s <= 3))
        def _():
            sent(wbit, s_ry.at[s, ch])

        @pl.when((s == 0) & (c != z))
        def _():
            sent(bit, s_root.at[ch])


def panels(trailing, n1, n2t):
    piece, width = n1.shape
    dma = pltpu.SemaphoreType.DMA
    vm = pltpu.VMEM
    scratch = [
        vm((8, piece, width), F32),
        vm((4, width, piece), F32),
        vm((4, width, piece), BF16),
        vm((4, width, piece), BF16),
        vm((4, piece, width), F32),
        vm((8, width, piece), F32),
        vm((5, width, piece), F32),
        vm((5, width, piece), F32),
        vm((4, width, piece), F32),
        vm((width, piece), F32),
        vm((2, 2 * piece, piece), F32),
        vm((piece, width), BF16),
        vm((piece, width), BF16),
        vm((2, piece, width), F32),
        vm((piece, width), F32),
        dma((8, CH)), dma((4,)), dma((5 * CH,)), dma((5 * CH,)), dma((4, CH)), dma((CH,)), dma((2,)), dma((2,)), dma((1,)),
        dma((5 * CH,)), dma((5 * CH,)), dma((4, CH)), dma((CH,)), dma((3,)), dma((4, CH)), dma((5 * CH,)), dma((2,)), dma((1,)),
    ]
    anyspace = pl.BlockSpec(memory_space=pl.ANY)
    inv = pl.BlockSpec(memory_space=pltpu.VMEM)
    return pl.pallas_call(
        panels_kernel,
        out_shape=(
            jax.ShapeDtypeStruct((piece, width), F32),
            jax.ShapeDtypeStruct((width, piece), F32),
        ),
        in_specs=[anyspace, anyspace, anyspace],
        out_specs=(inv, inv),
        scratch_shapes=scratch,
        compiler_params=pltpu.CompilerParams(
            collective_id=0, has_side_effects=True, vmem_limit_bytes=63 * 2**20
        ),
        name="panels",
    )(trailing, n1, n2t)


def column_panel(normal):
    rows, cols = lax.axis_size("row"), lax.axis_size("col")
    moves = [(p, (p % rows) * cols + p // rows) for p in range(rows * cols)]
    piece = lax.ppermute(normal, ("row", "col"), moves)
    return lax.all_gather(piece, "row", axis=0, tiled=True)


def total_over_all(x):
    return lax.psum(x, ("row", "col"))


def sweep(trailing, col_block):
    part = big_product(trailing, col_block)
    return lax.psum_scatter(part, "col", scatter_dimension=0, tiled=True)


def body(
    special,
    trailing,
    factor_one,
    inverse_one,
    factor_two_top,
    factor_two,
    inverse_two,
    structure_one,
    structure_two,
):
    piece_rows = factor_one.shape[0]
    row_index = lax.axis_index("row")
    col_index = lax.axis_index("col")
    first_row = (row_index * lax.axis_size("col") + col_index) * piece_rows
    mask_one = block_flags(structure_one, first_row, piece_rows)
    mask_two = block_flags(structure_two, first_row, piece_rows)
    normal_one = mask_one * product(factor_one, inverse_one)
    normal_two = mask_two * product(factor_two, inverse_two)
    normal_top = product(factor_two_top, inverse_two)
    if special:
        sum_one, sum_two = panels(trailing, normal_one, normal_two.T)
        sum_two = sum_two.T
    else:
        sum_one = sweep(trailing, column_panel(normal_one))
        sum_two = sweep(trailing, column_panel(normal_two))
    column_one = -mask_one * sum_one
    both = product(column_one.T, jnp.concatenate([normal_one, normal_two], axis=1))
    column_two = -mask_two * (sum_two + product(column_one, normal_top))
    second = product(normal_two.T, column_two)
    totals = total_over_all(jnp.concatenate([both, second], axis=1))
    width = normal_one.shape[1]
    diagonal_one = product(inverse_one.T, inverse_one) - totals[:, :width].T
    cross_two = -(product(diagonal_one, normal_top) + totals[:, width : 2 * width])
    diagonal_two = (
        product(inverse_two.T, inverse_two)
        - product(normal_top.T, cross_two)
        - totals[:, 2 * width :]
    )
    return (column_one, diagonal_one, column_two, cross_two, diagonal_two)


def solution(mesh):
    special = mesh.shape["row"] == 8 and mesh.shape["col"] == 4
    return jax.shard_map(
        functools.partial(body, special),
        mesh=mesh,
        in_specs=(
            P("row", "col"),
            P(("row", "col"), None),
            P(),
            P(),
            P(("row", "col"), None),
            P(),
            P(),
            P(),
        ),
        out_specs=(P(("row", "col"), None), P(), P(("row", "col"), None), P(), P()),
        check_vma=False,
    )
```

profile of v0, /device:TPU:0, one launch (start us, length us, event | category | flops | bytes accessed | tf_op | source)
XLA Modules:
  0.0 422.4 jit_solution(6502424480888068129)
XLA Ops:
  7.2 0.0 copy-start.1
  7.2 0.0 all-reduce.2.cloned.1.call-start
  7.3 0.9 compare_reduce_fusion.1
  8.2 0.8 compare_reduce_fusion
  9.0 3.4 convolution_multiply_fusion.1
  12.4 0.0 copy-start.7
  12.4 1.3 copy.22.n1_in
  13.7 2.8 fusion.11
  16.5 2.8 convolution_multiply_fusion
  19.4 225.0 %panels.1 = (f32[512,512]{1,0:T(8,128)}, f32[512,512]{1,0:T(8,128)}) custom-call(f32[2048,4096]{1,0:T(8,128)} %trail.1, f32[512,512]{1,0:T(8,128)} %copy.22.n1_in, f32[512,512]{1,0:T(8,128)} %bitcast.26), custom_call_target="tpu_custom_call" | custom-call | tf_op jit(solution)/shard_map/panels/pallas_call | solution.py:394
  244.4 1.4 broadcast_multiply_fusion
  245.8 0.0 copy-start.4
  245.8 0.0 copy-start.3
  245.8 5.4 %fusion = f32[512,1024]{0,1:T(8,128)S(1)} fusion(f32[512,512]{1,0:T(8,128)S(1)} %broadcast_multiply_fusion, f32[512,512]{0,1:T(8,128)} %convolution_multiply_fusion, f32[512,512]{0,1:T(8,128)} %copy-done.7), kind=kOutput, calls=%fused_computation.1 | convolution fusion | flops 3221749760 | bytes 5242880 | tf_op jit(solution)/shard_map/dot_general | solution.py:21
  251.2 0.0 copy-start
  251.3 1.9 fusion.6
  253.2 0.0 copy-start.5
  253.2 1.0 copy-done.5
  254.2 1.9 fusion.12
  256.1 2.0 pad_maximum_fusion
  258.1 0.0 all-reduce.2.cloned.1.call-update
  258.1 1.2 copy-done.6
  259.3 1.3 copy.28
  260.6 2.8 fusion.13
  263.4 136.7 %all-reduce.2.cloned.1.call-done = f32[512,1536]{0,1:T(8,128)} async-done(((f32[512,1536]{0,1:T(8,128)}), f32[512,1536]{0,1:T(8,128)}) %all-reduce.2.cloned.1.call-update) | async-done | bytes 3145744 | tf_op jit(solution)/shard_map/psum | solution.py:418
  400.1 3.3 convolution_subtract_fusion.1
  403.4 0.0 copy-start.10
  403.4 1.0 copy-done.10
  404.4 3.2 fusion.5
  407.6 1.3 copy.29
  408.9 4.1 fusion.4
  413.0 2.5 copy.30
  (23 shorter events, 0.1 us)
Async XLA Ops:
  7.2 6.5 %copy-start.1 = (f32[512,512]{1,0:T(8,128)S(1)}, f32[512,512]{1,0:T(8,128)}, u32[]{:S(2)}) copy-start(f32[512,512]{1,0:T(8,128)} %param.13) | copy-start | bytes 3145732
  7.2 6.5 %copy-start.11 = (f32[512,512]{1,0:T(8,128)S(1)}, f32[512,512]{1,0:T(8,128)}, u32[]{:S(2)}) copy-start(f32[512,512]{1,0:T(8,128)} %param.11) | copy-start | bytes 3145732
  7.2 392.9 %all-reduce.2.cloned.1.call-start = ((), (), s32[]{:S(2)}) async-start(), calls=%async_computation | async-start | bytes 6291456 | tf_op jit(solution)/shard_map/psum | solution.py:418
  12.4 7.0 %copy-start.7 = (f32[512,512]{0,1:T(8,128)}, f32[512,512]{0,1:T(8,128)S(1)}, u32[]{:S(2)}) copy-start(f32[512,512]{0,1:T(8,128)S(1)} %convolution_multiply_fusion.1) | copy-start | bytes 3145732
  13.7 2.8 copy-start.12
  245.8 7.5 %copy-start.4 = (f32[512,512]{1,0:T(8,128)}, f32[512,512]{1,0:T(8,128)S(1)}, u32[]{:S(2)}) copy-start(f32[512,512]{1,0:T(8,128)S(1)} %broadcast_multiply_fusion) | copy-start | bytes 3145732
  245.8 5.5 %copy-start.3 = (f32[512,512]{1,0:T(8,128)S(1)}, f32[512,512]{1,0:T(8,128)}, u32[]{:S(2)}) copy-start(f32[512,512]{1,0:T(8,128)} %fusion.11) | copy-start | bytes 3145732
  245.8 5.5 %copy-start.13 = (f32[512,512]{1,0:T(8,128)S(1)}, f32[512,512]{1,0:T(8,128)}, u32[]{:S(2)}) copy-start(f32[512,512]{1,0:T(8,128)} %get-tuple-element.8) | copy-start | bytes 3145732
  251.2 3.0 copy-start
  253.2 1.0 copy-start.5
  258.1 1.2 copy-start.6
  258.1 2.5 copy-start.2
  260.6 139.5 %copy-start.8 = (f32[512,512]{1,0:T(8,128)S(1)}, f32[512,512]{1,0:T(8,128)}, u32[]{:S(2)}) copy-start(f32[512,512]{1,0:T(8,128)} %param.10) | copy-start | bytes 3145732
  403.4 1.0 copy-start.10
  404.4 4.5 %copy-start.9 = (f32[512,512]{0,1:T(8,128)S(1)}, f32[512,512]{0,1:T(8,128)}, u32[]{:S(2)}) copy-start(f32[512,512]{0,1:T(8,128)} %fusion.13) | copy-start | bytes 3145732
Sparse Core Ops, SparseCore 0:
  258.2 141.8 all-reduce.1
where the time goes:
time: 423 us; the launch traced here: 422 us
  Pallas kernels  225 us (53%)
  waiting for transfers between devices  137 us (32%)
  matrix products  31.7 us (7%)
  between operations  14.2 us (3%)
  local copies, waits for them, and re-layouts  9.63 us (2%)
  other arithmetic  5.04 us (1%)
    pallas_call x1, Pallas kernels, panels(): pl.pallas_call(panels_kernel, out_shape=(jax.ShapeDtypeStruct((piece, wid...  225 us
    psum x1, waiting for transfers between devices, total_over_all(): return lax.psum(x, ('row', 'col'))  137 us
    dot_general x10, matrix products, product(): jnp.dot(left, right, precision=lax.Precision.HIGHEST, preferred_element_t...  31.7 us
  transfers between devices with their start and end apart: 1, of which 1 were waited for; matrix products, arithmetic and copies ran while one was open for 1% of the time, Pallas kernels for 0%

commit v1 on v0

--- a/solution.py
+++ b/solution.py
@@ -407,6 +407,117 @@
     )(trailing, n1, n2t)
 
 
+def total_kernel(s_in, out, acc, got1, got2, got3, got4, sem1, sem2, sem3, sem4, sem5, sem6, sem7, sem8, s_sem, z_send, z_send2):
+    r, c = lax.axis_index("row"), lax.axis_index("col")
+    z, y, x, k = r // 2, r % 2, c // 2, c % 2
+    ypart = (r + 1 - 2 * y, c)
+    cpart = (r, flip(c, 1))
+    xpart = (r, flip(c, 2))
+    rows = s_in.shape[1]
+    h1, h2, h3, h4 = rows // 2, rows // 4, rows // 8, rows // 32
+
+    def remote(src, dst, send, recv, to):
+        return pltpu.make_async_remote_copy(
+            src_ref=src, dst_ref=dst, send_sem=send, recv_sem=recv, device_id=to, device_id_type=MESH
+        )
+
+    def span(start, size):
+        return pl.ds(pl.multiple_of(start, size), size)
+
+    bar = pltpu.get_barrier_semaphore()
+    line = [(lax.rem(r + 2 * d, 8), c) for d in (1, 2, 3)]
+    for to in [ypart, cpart, xpart] + line:
+        pl.semaphore_signal(bar, inc=1, device_id=to, device_id_type=MESH)
+    pl.semaphore_wait(bar, 6)
+
+    sends = []
+
+    def exchange(pairs):
+        copies = [remote(*p) for p in pairs]
+        for cp in copies:
+            cp.start()
+        for cp in copies:
+            cp.wait_recv()
+        sends.extend(copies)
+
+    base = k * h1
+    exchange([(s_in.at[i, span((1 - k) * h1, h1)], got1.at[i], s_sem.at[0, i], sem1.at[i], cpart) for i in (0, 1)])
+    for i in (0, 1):
+        acc[i] = s_in[i, span(base, h1)] + got1[i]
+    first = (x, y)
+    second = (y, x)
+    one = (xpart, ypart)
+    two = (ypart, xpart)
+    exchange([(acc.at[i, span((1 - first[i]) * h2, h2)], got2.at[i], s_sem.at[1, i], sem2.at[i], one[i]) for i in (0, 1)])
+    at1 = [first[i] * h2 for i in (0, 1)]
+    for i in (0, 1):
+        acc[i, span(at1[i], h2)] += got2[i]
+    exchange(
+        [
+            (acc.at[i, span(at1[i] + (1 - second[i]) * h3, h3)], got3.at[i], s_sem.at[2, i], sem3.at[i], two[i])
+            for i in (0, 1)
+        ]
+    )
+    at2 = [at1[i] + second[i] * h3 for i in (0, 1)]
+    for i in (0, 1):
+        acc[i, span(at2[i], h3)] += got3[i]
+    pairs = []
+    for d in (1, 2, 3):
+        to_z = lax.rem(z + d, 4)
+        for i in (0, 1):
+            pairs.append(
+                (acc.at[i, span(at2[i] + to_z * h4, h4)], got4.at[d - 1, i], z_send.at[d - 1, i], sem4.at[d - 1, i], line[d - 1])
+            )
+    exchange(pairs)
+    pairs = []
+    for i in (0, 1):
+        mine = acc[i, span(at2[i] + z * h4, h4)] + got4[0, i] + (got4[1, i] + got4[2, i])
+        place = span(base + at2[i] + z * h4, h4)
+        out[i, place] = mine
+    for d in (1, 2, 3):
+        for i in (0, 1):
+            place = span(base + at2[i] + z * h4, h4)
+            pairs.append((out.at[i, place], out.at[i, place], z_send2.at[d - 1, i], sem5.at[d - 1, i], line[d - 1]))
+    exchange(pairs)
+    places = [span(base + at2[i], h3) for i in (0, 1)]
+    exchange([(out.at[i, places[i]], out.at[i, places[i]], s_sem.at[3, i], sem6.at[i], two[i]) for i in (0, 1)])
+    places = [span(base + at1[i], h2) for i in (0, 1)]
+    exchange([(out.at[i, places[i]], out.at[i, places[i]], s_sem.at[4, i], sem7.at[i], one[i]) for i in (0, 1)])
+    place = span(base, h1)
+    exchange([(out.at[i, place], out.at[i, place], s_sem.at[5, i], sem8.at[i], cpart) for i in (0, 1)])
+    for cp in sends:
+        cp.wait_send()
+
+
+def total_special(x):
+    rows, cols = x.shape
+    stacked = jnp.stack([x[:, : cols // 2], x[:, cols // 2 :]])
+    w = cols // 2
+    dma = pltpu.SemaphoreType.DMA
+    vm = pltpu.VMEM
+    inv = pl.BlockSpec(memory_space=pltpu.VMEM)
+    out = pl.pallas_call(
+        total_kernel,
+        out_shape=jax.ShapeDtypeStruct((2, rows, w), F32),
+        in_specs=[inv],
+        out_specs=inv,
+        scratch_shapes=[
+            vm((2, rows // 2, w), F32),
+            vm((2, rows // 2, w), F32),
+            vm((2, rows // 4, w), F32),
+            vm((2, rows // 8, w), F32),
+            vm((3, 2, rows // 32, w), F32),
+            dma((2,)), dma((2,)), dma((2,)), dma((3, 2)), dma((3, 2)), dma((2,)), dma((2,)), dma((2,)),
+            dma((6, 2)), dma((3, 2)), dma((3, 2)),
+        ],
+        compiler_params=pltpu.CompilerParams(
+            collective_id=1, has_side_effects=True, vmem_limit_bytes=40 * 2**20
+        ),
+        name="total",
+    )(stacked)
+    return jnp.concatenate([out[0], out[1]], axis=1)
+
+
 def column_panel(normal):
     rows, cols = lax.axis_size("row"), lax.axis_size("col")
     moves = [(p, (p % rows) * cols + p // rows) for p in range(rows * cols)]
@@ -453,7 +564,7 @@
     both = product(column_one.T, jnp.concatenate([normal_one, normal_two], axis=1))
     column_two = -mask_two * (sum_two + product(column_one, normal_top))
     second = product(normal_two.T, column_two)
-    totals = total_over_all(jnp.concatenate([both, second], axis=1))
+    totals = (total_special if special else total_over_all)(jnp.concatenate([both, second], axis=1))
     width = normal_one.shape[1]
     diagonal_one = product(inverse_one.T, inverse_one) - totals[:, :width].T
     cross_two = -(product(diagonal_one, normal_top) + totals[:, width : 2 * width])

time: 423 us -> 327 us (0.77)
  waiting for transfers between devices: 137 us -> 0 us
  Pallas kernels: 225 us -> 286 us
  between operations: 14.2 us -> 0.94 us
  matrix products: 31.7 us -> 27.4 us
    psum x1 -> x0, waiting for transfers between devices: 137 us -> none  [total_over_all(): return lax.psum(x, ('row', 'col'))]
    pallas_call x0 -> x1, Pallas kernels: none -> 61.2 us  [total_special(): pl.pallas_call(total_kernel, out_shape=jax.ShapeDtypeStruct((2, rows, w),...]
    dot_general x10, matrix products: 31.7 us -> 27.4 us  [product(): jnp.dot(left, right, precision=lax.Precision.HIGHEST, preferred_element_t...]
  transfers between devices with their start and end apart: 1 -> 0, of which waited for: 1 -> 0; matrix products, arithmetic and copies ran while one was open for 1% -> 0% of each run, Pallas kernels for 0% -> 0%
where the time goes in v1:
time: 327 us; the launch traced here: 324 us
  Pallas kernels  286 us (87%)
  matrix products  27.4 us (8%)
  local copies, waits for them, and re-layouts  6.43 us (2%)
    pallas_call x1, Pallas kernels, panels(): pl.pallas_call(panels_kernel, out_shape=(jax.ShapeDtypeStruct((piece, wid...  225 us
    pallas_call x1, Pallas kernels, total_special(): pl.pallas_call(total_kernel, out_shape=jax.ShapeDtypeStruct((2, rows, w),...  61.2 us
    dot_general x10, matrix products, product(): jnp.dot(left, right, precision=lax.Precision.HIGHEST, preferred_element_t...  27.4 us

profile of v1, /device:TPU:0, one launch (start us, length us, event | category | flops | bytes accessed | tf_op | source)
XLA Modules:
  0.0 323.8 jit_solution(8332250931820247259)
XLA Ops:
  0.7 0.8 compare_reduce_fusion
  1.4 0.0 copy-start.11
  1.4 0.0 copy-start.5
  1.5 0.0 copy-start.9
  1.5 4.5 %convolution_multiply_fusion = f32[512,512]{0,1:T(8,128)} fusion(f32[512,512]{1,0:T(8,128)} %param.12, f32[512,512]{1,0:T(8,128)} %param.13, f32[512]{0:T(512)S(1)} %convert_element_type.21), kind=kOutput, calls=%fused_computation.17 | convolution fusion | flops 1610874880 | bytes 3147776 | tf_op jit(solution)/shard_map/dot_general | solution.py:21
  6.0 0.1 compare_reduce_fusion.1
  6.1 1.9 convolution_multiply_fusion.1
  8.0 0.0 copy-start.3
  8.0 1.0 copy-done.3
  9.0 1.3 copy.19.n1_in
  10.3 225.0 %panels.1 = (f32[512,512]{1,0:T(8,128)}, f32[512,512]{1,0:T(8,128)}) custom-call(f32[2048,4096]{1,0:T(8,128)} %trail.1, f32[512,512]{1,0:T(8,128)} %copy.19.n1_in, f32[512,512]{1,0:T(8,128)} %bitcast.34), custom_call_target="tpu_custom_call" | custom-call | tf_op jit(solution)/shard_map/panels/pallas_call | solution.py:394
  235.3 0.0 copy-start.1
  235.3 0.0 copy-start.8
  235.3 1.5 broadcast_multiply_fusion
  236.8 0.0 copy-start.2
  236.9 0.3 copy-done.8
  237.2 1.8 fusion.12
  239.0 1.9 fusion.7
  240.9 0.0 copy-start.4
  240.9 1.9 fusion.13
  242.8 7.0 %fusion = f32[512,1024]{1,0:T(8,128)S(1)} fusion(f32[512,512]{1,0:T(8,128)S(1)} %broadcast_multiply_fusion, f32[512,512]{0,1:T(8,128)S(1)} %copy-done, f32[512,512]{0,1:T(8,128)S(1)} %copy-done.4), kind=kOutput, calls=%fused_computation.1 | convolution fusion | flops 3221749760 | bytes 5242880 | tf_op jit(solution)/shard_map/dot_general | solution.py:21
  249.8 0.3 slice_bitcast_fusion
  250.1 0.2 pad_maximum_fusion.s_in
  250.3 61.2 %total.1 = f32[2,512,768]{2,1,0:T(8,128)S(1)} custom-call(f32[2,512,768]{2,1,0:T(8,128)S(1)} %pad_maximum_fusion.s_in), custom_call_target="tpu_custom_call" | custom-call | tf_op jit(solution)/shard_map/total/pallas_call | solution.py:499
  311.5 0.2 slice_bitcast_fusion.1
  311.7 1.0 copy-done.6
  312.7 1.9 convolution_subtract_fusion.1
  314.6 1.9 fusion.6
  316.5 1.9 fusion.14
  318.3 2.8 fusion.5
  321.2 1.3 copy.23
  322.5 1.3 copy.24
  (18 shorter events, 0.1 us)
Async XLA Ops:
  1.4 4.6 %copy-start.11 = (s32[96]{0:T(128)S(1)}, s32[96]{0:T(128)}, u32[]{:S(2)}) copy-start(s32[96]{0:T(128)} %param.14) | copy-start | bytes 1156
  1.4 4.7 %copy-start.5 = (f32[512,512]{1,0:T(8,128)S(1)}, f32[512,512]{1,0:T(8,128)}, u32[]{:S(2)}) copy-start(f32[512,512]{1,0:T(8,128)} %param.10) | copy-start | bytes 3145732
  1.5 4.7 %copy-start.9 = (f32[512,512]{1,0:T(8,128)S(1)}, f32[512,512]{1,0:T(8,128)}, u32[]{:S(2)}) copy-start(f32[512,512]{1,0:T(8,128)} %param.9) | copy-start | bytes 3145732
  8.0 1.0 copy-start.3
  235.3 1.6 copy-start.1
  235.3 1.8 copy-start.8
  236.8 6.0 %copy-start.2 = (f32[512,512]{1,0:T(8,128)}, f32[512,512]{1,0:T(8,128)S(1)}, u32[]{:S(2)}) copy-start(f32[512,512]{1,0:T(8,128)S(1)} %broadcast_multiply_fusion) | copy-start | bytes 3145732
  237.2 1.9 copy-start.10
  239.0 1.9 copy-start
  240.9 1.9 copy-start.4
  311.5 1.2 copy-start.6
  316.4 1.9 copy-start.7

commit v2 on v0

--- a/solution.py
+++ b/solution.py
@@ -10,9 +10,18 @@
 BLK = 128
 MESH = pl.DeviceIdType.MESH
 CH = 8
-LAG = 2
-RS0 = 9
-A0 = 23
+AG_LAG = 1
+RS_LAG = 4
+RS0 = 10
+Y0 = 9
+Y_RATE = 2
+ROOT_RATE = 2
+AG_O, AG_T = (0, 0, 0, 0, 1), (1, 0, 2, 3, 0)
+RS_O, RS_T = (1, 0, 0, 0, 0), (0, 3, 2, 1, 0)
+B_O, B_T = (1, 1, 0, 1, 0, 1, 0, 0), (0, 3, 3, 2, 2, 1, 1, 0)
+A_O, A_T = (0, 0, 1, 0, 0, 1, 1, 1), (1, 0, 1, 2, 3, 2, 0, 3)
+Y_T = (3, 2, 1)
+A_TICK = (16, 17, 19, 20, 21, 22, 27, 28, 35, 36, 37, 38, 43, 44, 45, 46)
 F32 = jnp.float32
 BF16 = jnp.bfloat16
 
@@ -40,14 +49,24 @@
     return jnp.dot(left, right, preferred_element_type=F32)
 
 
+def mm3(left, right):
+    lh, ll = split(left)
+    rh, rl = split(right)
+    return mm(lh, rh) + (mm(ll, rh) + mm(lh, rl))
+
+
 def flip(c, t):
     return ((c // 2 + t // 2) % 2) * 2 + (c % 2 + t % 2) % 2
 
 
+def pick(table, index):
+    return sum(jnp.where(index == i, v, 0) for i, v in enumerate(table) if v)
+
+
 def panels_kernel(
-    trail, n1_in, n2_in, y1_out, y2_out,
+    trail, f1, inv1, f2, inv2, mask1, mask2, y1_out, y2_out, n1_in, n2_in,
     n1buf, n2buf, n2h, n2l, out1, out2, rsu, rsd, rsy, y2buf, tbuf, n1h, n1l, cbuf, xbuf,
-    ag_sem, n2_sem, up_sem, dn_sem, ry_sem, y2_sem, t_sem, c_sem, x_sem,
+    f_sem, ag_sem, n2_sem, up_sem, dn_sem, ry_sem, y2_sem, t_sem, c_sem, x_sem,
     s_up, s_dn, s_y, s_root, s_n2, s_ry, s_line, s_c, s_x,
 ):
     r, c = lax.axis_index("row"), lax.axis_index("col")
@@ -85,13 +104,10 @@
     def tile_of(u):
         isa = u // 16
         v = u % 16
-        p = v % 8
-        tb = (4 - (p + 1) // 2) % 4
-        ob = p % 2 + (7 - p) // 7 - p // 7
-        hb = (x + v // 8) % 2
-        ta, oa, ha = v // 4, (v // 2) % 2, v % 2
-        t = isa * ta + (1 - isa) * tb
-        o = isa * oa + (1 - isa) * ob
+        hb, ha = (x + v // 8) % 2, v % 2
+        pb, pa = v % 8, v // 2
+        t = isa * pick(A_T, pa) + (1 - isa) * pick(B_T, pb)
+        o = isa * pick(A_O, pa) + (1 - isa) * pick(B_O, pb)
         h = isa * ha + (1 - isa) * hb
         return ((y + o) % 2) * 4 + flip(c, t), h, t, o
 
@@ -104,6 +120,12 @@
         return pltpu.make_async_copy(trail.at[rows, cols], tbuf.at[u % 2], t_sem.at[u % 2])
 
     fetch(0).start()
+    loads = [pltpu.make_async_copy(a, out2.at[i], f_sem.at[i]) for i, a in enumerate((f2, inv2, f1, inv1))]
+    for cp in loads:
+        cp.start()
+    loads[0].wait()
+    loads[1].wait()
+    n2_in[...] = (mask2[...] * mm3(out2[0], out2[1])).T
     own = pltpu.make_async_copy(n2_in, n2buf.at[c], n2_sem.at[0])
     own.start()
 
@@ -114,6 +136,9 @@
     to_c = remote(n2_in, n2buf.at[c], s_n2.at[1], n2_sem.at[1], cpart)
     to_c.start()
 
+    loads[2].wait()
+    loads[3].wait()
+    n1_in[...] = mask1[...] * mm3(out2[2], out2[3])
     here = y * 4 + c
     for ch in range(CH):
         part = pl.ds(ch * cr, cr)
@@ -134,8 +159,7 @@
 
     def ag_step(n):
         s, ch = n // CH, n % CH
-        o = (s + 3) // 4 - (s + 2) // 4
-        t = s - (s + 3) // 4
+        o, t = pick(AG_O, s), pick(AG_T, s)
         j = ((y + o) % 2) * 4 + flip(c, t)
         part = pl.ds(pl.multiple_of(ch * cr, cr), cr)
         chunk = n1buf.at[j, part]
@@ -149,15 +173,14 @@
         def _():
             remote(chunk, chunk, s_dn.at[n], ag_sem.at[j, ch], below).start()
 
-        @pl.when((s >= 2) | ((s == 0) & (z == c)))
+        @pl.when((o == 0) & ((t > 0) | (z == c)))
         def _():
             remote(chunk, chunk, s_y.at[t, ch], ag_sem.at[j, ch], ypart).start()
 
     def rs_step(n):
         s, ch = n // CH, n % CH
-        mine = (s + 3) // 4
-        t = (4 - s) * mine
-        j = ((y + 1 - mine) % 2) * 4 + flip(c, t)
+        o, t = pick(RS_O, s), pick(RS_T, s)
+        j = ((y + o) % 2) * 4 + flip(c, t)
         part = pl.ds(pl.multiple_of(ch * wr, wr), wr)
         chunk = out2.at[j, part]
 
@@ -171,7 +194,7 @@
             arrived(rsd.at[s, part], dn_sem.at[n])
             chunk[...] += rsd[s, part]
 
-        @pl.when(((s >= 1) & (s <= 3)) | ((s == 4) & (z == c)))
+        @pl.when((o == 0) & ((t > 0) | (z == c)))
         def _():
             arrived(rsy.at[t, part], ry_sem.at[t, ch])
             chunk[...] += rsy[t, part]
@@ -184,15 +207,15 @@
         def _():
             remote(chunk, rsd.at[s, part], s_line.at[n], dn_sem.at[n], above).start()
 
-        @pl.when((z == c) & (s == 0))
+        @pl.when((z == c) & (o == 1))
         def _():
             remote(chunk, rsy.at[0, part], s_line.at[n], ry_sem.at[0, ch], ypart).start()
 
-        @pl.when((z == c) & (s >= 1) & (s <= 3))
+        @pl.when((z == c) & (o == 0) & (t > 0))
         def _():
             remote(chunk, y2buf.at[part], s_line.at[n], y2_sem.at[ch], (r, flip(c, t))).start()
 
-        @pl.when((z == c) & (s == 4))
+        @pl.when((z == c) & (o == 0) & (t == 0))
         def _():
             pltpu.make_async_copy(chunk, y2buf.at[part], y2_sem.at[ch]).start()
 
@@ -216,11 +239,11 @@
             def _():
                 out2[j] += add
 
-        @pl.when((u >= 8) & (o == 1) & (t >= 1))
-        def _():
-            for ch in range(CH):
-                part = pl.ds(ch * wr, wr)
-                remote(out2.at[j, part], rsy.at[t, part], s_ry.at[t, ch], ry_sem.at[t, ch], ypart).start()
+    def y_step(q):
+        t, ch = pick(Y_T, q // CH), q % CH
+        part = pl.ds(pl.multiple_of(ch * wr, wr), wr)
+        j = ((y + 1) % 2) * 4 + flip(c, t)
+        remote(out2.at[j, part], rsy.at[t, part], s_ry.at[t, ch], ry_sem.at[t, ch], ypart).start()
 
     def turn_a(u):
         j, h, t, o = tile_of(u)
@@ -256,9 +279,10 @@
                 out1[q] += add
 
     qx = flip(c, 2)
-    end_a = A0 + 28
-    ag_first = LAG * dist
-    rs_first = RS0 + LAG * jnp.where(z > c, 3 - z, jnp.where(z < c, z, jnp.where(c < 2, 3 - c, c)))
+    end_a = A_TICK[15] + 1
+    ag_first = AG_LAG * dist
+    ag_rate = jnp.where(z == c, ROOT_RATE, 1)
+    rs_first = RS0 + RS_LAG * jnp.where(z > c, 3 - z, jnp.where(z < c, z, jnp.where(c < 2, 3 - c, c)))
 
     def core_copy(i):
         to = flip(c, 1 + 2 * (1 - i))
@@ -267,11 +291,13 @@
     x_copy = remote(out1.at[qx], xbuf, s_x.at[0], x_sem.at[0], xpart)
 
     def tick(step, carry):
-        n = step - ag_first
-
-        @pl.when((n >= 0) & (n < 5 * CH))
-        def _():
-            ag_step(n)
+        @pl.loop(0, ag_rate)
+        def _(i):
+            n = (step - ag_first) * ag_rate + i
+
+            @pl.when((n >= 0) & (n < 5 * CH))
+            def _():
+                ag_step(n)
 
         m = step - rs_first
 
@@ -294,11 +320,16 @@
         def _():
             turn_b(step)
 
-        w = step - A0
-
-        @pl.when((w >= 0) & (w < 32) & (w % 8 < 4))
-        def _():
-            turn_a(16 + (w // 8) * 4 + w % 4)
+        for i in range(Y_RATE):
+            q = (step - Y0) * Y_RATE + i
+
+            @pl.when((q >= 0) & (q < 3 * CH))
+            def _():
+                y_step(q)
+
+        @pl.when(sum(jnp.where(step == a, 1, 0) for a in A_TICK) > 0)
+        def _():
+            turn_a(15 + sum(jnp.where(step >= a, 1, 0) for a in A_TICK))
 
         @pl.when(step == end_a)
         def _():
@@ -315,7 +346,7 @@
 
         return carry
 
-    last_tick = RS0 + 3 * LAG + 5 * CH
+    last_tick = RS0 + 3 * RS_LAG + 5 * CH
     lax.fori_loop(0, max(last_tick, end_a + 2), tick, 0)
 
     x_copy.wait_recv()
@@ -349,25 +380,27 @@
         def _():
             sent(bit, s_dn.at[n])
 
-        @pl.when((s >= 2) | ((s == 0) & (z == c)))
-        def _():
-            sent(bit, s_y.at[s - (s + 3) // 4, ch])
-
-        @pl.when((z != c) | (s < 4))
+        o, t = pick(AG_O, s), pick(AG_T, s)
+
+        @pl.when((o == 0) & ((t > 0) | (z == c)))
+        def _():
+            sent(bit, s_y.at[t, ch])
+
+        @pl.when((z != c) | (pick(RS_O, s) == 1) | (pick(RS_T, s) > 0))
         def _():
             sent(wbit, s_line.at[n])
 
-        @pl.when((s >= 1) & (s <= 3))
-        def _():
-            sent(wbit, s_ry.at[s, ch])
+        @pl.when(s < 3)
+        def _():
+            sent(wbit, s_ry.at[s + 1, ch])
 
         @pl.when((s == 0) & (c != z))
         def _():
             sent(bit, s_root.at[ch])
 
 
-def panels(trailing, n1, n2t):
-    piece, width = n1.shape
+def panels(trailing, f1, inv1, f2, inv2, mask1, mask2):
+    piece, width = f1.shape
     dma = pltpu.SemaphoreType.DMA
     vm = pltpu.VMEM
     scratch = [
@@ -386,7 +419,7 @@
         vm((piece, width), BF16),
         vm((2, piece, width), F32),
         vm((piece, width), F32),
-        dma((8, CH)), dma((4,)), dma((5 * CH,)), dma((5 * CH,)), dma((4, CH)), dma((CH,)), dma((2,)), dma((2,)), dma((1,)),
+        dma((4,)), dma((8, CH)), dma((4,)), dma((5 * CH,)), dma((5 * CH,)), dma((4, CH)), dma((CH,)), dma((2,)), dma((2,)), dma((1,)),
         dma((5 * CH,)), dma((5 * CH,)), dma((4, CH)), dma((CH,)), dma((3,)), dma((4, CH)), dma((5 * CH,)), dma((2,)), dma((1,)),
     ]
     anyspace = pl.BlockSpec(memory_space=pl.ANY)
@@ -396,15 +429,171 @@
         out_shape=(
             jax.ShapeDtypeStruct((piece, width), F32),
             jax.ShapeDtypeStruct((width, piece), F32),
-        ),
-        in_specs=[anyspace, anyspace, anyspace],
-        out_specs=(inv, inv),
+        )
+        * 2,
+        in_specs=[anyspace] * 5 + [inv, inv],
+        out_specs=(inv,) * 4,
         scratch_shapes=scratch,
         compiler_params=pltpu.CompilerParams(
             collective_id=0, has_side_effects=True, vmem_limit_bytes=63 * 2**20
         ),
         name="panels",
-    )(trailing, n1, n2t)
+    )(trailing, f1, inv1, f2, inv2, mask1, mask2)
+
+
+def finish_kernel(
+    y1, y2t, n1, n2t, mask1, mask2, inv1, inv2, f_top,
+    col1, diag1, col2, cross2, diag2,
+    part0, part1, part2, sum0, sum1, sum2, top, top_t, square1, square2,
+    acc, got1, got2, got3, got4, recv, send, z_recv, z_send, z_back, z_out,
+):
+    parts, outs = (part0, part1, part2), (sum0, sum1, sum2)
+    r, c = lax.axis_index("row"), lax.axis_index("col")
+    z, y, x, k = r // 2, r % 2, c // 2, c % 2
+    ypart = (r + 1 - 2 * y, c)
+    cpart = (r, flip(c, 1))
+    xpart = (r, flip(c, 2))
+    rows, cols = parts[0].shape
+    h1, h2, h3, h4 = rows // 2, rows // 4, rows // 8, rows // 32
+    side = [pl.ds(0, cols // 2), pl.ds(cols // 2, cols // 2)]
+    first, second = (x, y), (y, x)
+    one, two = (xpart, ypart), (ypart, xpart)
+    base = k * h1
+    at1 = [first[i] * h2 for i in (0, 1)]
+    at2 = [at1[i] + second[i] * h3 for i in (0, 1)]
+    line = [(lax.rem(r + 2 * d, 8), c) for d in (1, 2, 3)]
+
+    def remote(src, dst, s_sem, r_sem, to):
+        return pltpu.make_async_remote_copy(
+            src_ref=src, dst_ref=dst, send_sem=s_sem, recv_sem=r_sem, device_id=to, device_id_type=MESH
+        )
+
+    def span(start, size):
+        return pl.ds(pl.multiple_of(start, size), size)
+
+    bar = pltpu.get_barrier_semaphore()
+    for to in [ypart, cpart, xpart] + line:
+        pl.semaphore_signal(bar, inc=1, device_id=to, device_id_type=MESH)
+    pl.semaphore_wait(bar, 6)
+
+    def copies(m, stage):
+        if stage == 0:
+            return [remote(parts[m].at[span((1 - k) * h1, h1)], got1.at[m], send.at[m, 0, 0], recv.at[m, 0, 0], cpart)]
+        if stage == 1:
+            return [
+                remote(acc.at[m, span((1 - first[i]) * h2, h2), side[i]], got2.at[m, i], send.at[m, 1, i], recv.at[m, 1, i], one[i])
+                for i in (0, 1)
+            ]
+        if stage == 2:
+            return [
+                remote(
+                    acc.at[m, span(at1[i] + (1 - second[i]) * h3, h3), side[i]],
+                    got3.at[m, i], send.at[m, 2, i], recv.at[m, 2, i], two[i],
+                )
+                for i in (0, 1)
+            ]
+        if stage == 3:
+            return [
+                remote(
+                    acc.at[m, span(at2[i] + lax.rem(z + d, 4) * h4, h4), side[i]],
+                    got4.at[m, d - 1, i], z_send.at[m, d - 1, i], z_recv.at[m, d - 1, i], line[d - 1],
+                )
+                for d in (1, 2, 3)
+                for i in (0, 1)
+            ]
+        if stage == 4:
+            places = [outs[m].at[span(base + at2[i] + z * h4, h4), side[i]] for i in (0, 1)]
+            return [
+                remote(places[i], places[i], z_out.at[m, d - 1, i], z_back.at[m, d - 1, i], line[d - 1])
+                for d in (1, 2, 3)
+                for i in (0, 1)
+            ]
+        if stage == 7:
+            place = outs[m].at[span(base, h1)]
+            return [remote(place, place, send.at[m, 5, 0], recv.at[m, 5, 0], cpart)]
+        to = (two, one)[stage - 5]
+        size, at = ((h3, at2), (h2, at1))[stage - 5]
+        places = [outs[m].at[span(base + at[i], size), side[i]] for i in (0, 1)]
+        return [remote(places[i], places[i], send.at[m, stage - 2, i], recv.at[m, stage - 2, i], to[i]) for i in (0, 1)]
+
+    def take(m, stage):
+        for cp in copies(m, stage):
+            cp.wait_recv()
+        if stage == 0:
+            acc[m] = parts[m][span(base, h1)] + got1[m]
+        for i in (0, 1):
+            if stage == 1:
+                acc[m, span(at1[i], h2), side[i]] += got2[m, i]
+            if stage == 2:
+                acc[m, span(at2[i], h3), side[i]] += got3[m, i]
+            if stage == 3:
+                mine = acc[m, span(at2[i] + z * h4, h4), side[i]] + got4[m, 0, i] + (got4[m, 1, i] + got4[m, 2, i])
+                outs[m][span(base + at2[i] + z * h4, h4), side[i]] = mine
+
+    def make(m):
+        if m == 0:
+            col1[...] = -mask1[...] * y1[...]
+            part0[...] = mm3(n1[...].T, col1[...])
+        if m == 1:
+            part1[...] = mm3(n2t[...], col1[...])
+            top[...] = mm3(f_top[...], inv2[...])
+        if m == 2:
+            col2[...] = -mask2[...] * (y2t[...].T + mm3(col1[...], top[...]))
+            part2[...] = mm3(n2t[...], col2[...])
+
+    for step in range(8 + 3):
+        if step == 3:
+            square1[...] = mm3(inv1[...].T, inv1[...])
+        if step == 4:
+            square2[...] = mm3(inv2[...].T, inv2[...])
+        if step == 5:
+            top_t[...] = top[...].T
+        for m in range(3):
+            stage = step - m
+            if stage == 0:
+                make(m)
+            if 1 <= stage <= 8:
+                take(m, stage - 1)
+            if 0 <= stage < 8:
+                for cp in copies(m, stage):
+                    cp.start()
+        if step == 9:
+            diag1[...] = square1[...] - sum0[...]
+            cross2[...] = -(mm3(diag1[...], top[...]) + sum1[...].T)
+            square2[...] -= mm3(top_t[...], cross2[...])
+    diag2[...] = square2[...] - sum2[...]
+    for m in range(3):
+        for stage in range(8):
+            for cp in copies(m, stage):
+                cp.wait_send()
+
+
+def finish(y1, y2t, n1, n2t, mask1, mask2, inv1, inv2, f_top):
+    rows, cols = y1.shape
+    w = cols // 2
+    dma = pltpu.SemaphoreType.DMA
+    vm = pltpu.VMEM
+    inv = pl.BlockSpec(memory_space=pltpu.VMEM)
+    return pl.pallas_call(
+        finish_kernel,
+        out_shape=(jax.ShapeDtypeStruct((rows, cols), F32),) * 5,
+        in_specs=[inv] * 9,
+        out_specs=(inv,) * 5,
+        scratch_shapes=[
+            *[vm((rows, cols), F32)] * 10,
+            vm((3, rows // 2, cols), F32),
+            vm((3, rows // 2, cols), F32),
+            vm((3, 2, rows // 4, w), F32),
+            vm((3, 2, rows // 8, w), F32),
+            vm((3, 3, 2, rows // 32, w), F32),
+            dma((3, 6, 2)), dma((3, 6, 2)),
+            dma((3, 3, 2)), dma((3, 3, 2)), dma((3, 3, 2)), dma((3, 3, 2)),
+        ],
+        compiler_params=pltpu.CompilerParams(
+            collective_id=1, has_side_effects=True, vmem_limit_bytes=60 * 2**20
+        ),
+        name="finish",
+    )(y1, y2t, n1, n2t, mask1, mask2, inv1, inv2, f_top)
 
 
 def column_panel(normal):
@@ -412,10 +601,6 @@
     moves = [(p, (p % rows) * cols + p // rows) for p in range(rows * cols)]
     piece = lax.ppermute(normal, ("row", "col"), moves)
     return lax.all_gather(piece, "row", axis=0, tiled=True)
-
-
-def total_over_all(x):
-    return lax.psum(x, ("row", "col"))
 
 
 def sweep(trailing, col_block):
@@ -440,28 +625,23 @@
     first_row = (row_index * lax.axis_size("col") + col_index) * piece_rows
     mask_one = block_flags(structure_one, first_row, piece_rows)
     mask_two = block_flags(structure_two, first_row, piece_rows)
+    if special and piece_rows == factor_one.shape[1]:
+        sums = panels(trailing, factor_one, inverse_one, factor_two, inverse_two, mask_one, mask_two)
+        return finish(*sums, mask_one, mask_two, inverse_one, inverse_two, factor_two_top)
     normal_one = mask_one * product(factor_one, inverse_one)
     normal_two = mask_two * product(factor_two, inverse_two)
     normal_top = product(factor_two_top, inverse_two)
-    if special:
-        sum_one, sum_two = panels(trailing, normal_one, normal_two.T)
-        sum_two = sum_two.T
-    else:
-        sum_one = sweep(trailing, column_panel(normal_one))
-        sum_two = sweep(trailing, column_panel(normal_two))
-    column_one = -mask_one * sum_one
-    both = product(column_one.T, jnp.concatenate([normal_one, normal_two], axis=1))
-    column_two = -mask_two * (sum_two + product(column_one, normal_top))
-    second = product(normal_two.T, column_two)
-    totals = total_over_all(jnp.concatenate([both, second], axis=1))
-    width = normal_one.shape[1]
-    diagonal_one = product(inverse_one.T, inverse_one) - totals[:, :width].T
-    cross_two = -(product(diagonal_one, normal_top) + totals[:, width : 2 * width])
-    diagonal_two = (
-        product(inverse_two.T, inverse_two)
-        - product(normal_top.T, cross_two)
-        - totals[:, 2 * width :]
+    column_one = -mask_one * sweep(trailing, column_panel(normal_one))
+    column_two = -mask_two * (sweep(trailing, column_panel(normal_two)) + product(column_one, normal_top))
+    parts = (
+        product(normal_one.T, column_one),
+        product(column_one.T, normal_two),
+        product(normal_two.T, column_two),
     )
+    first, cross, second = lax.psum(parts, ("row", "col"))
+    diagonal_one = product(inverse_one.T, inverse_one) - first
+    cross_two = -(product(diagonal_one, normal_top) + cross)
+    diagonal_two = product(inverse_two.T, inverse_two) - product(normal_top.T, cross_two) - second
     return (column_one, diagonal_one, column_two, cross_two, diagonal_two)
 
 

time: 423 us -> 267 us (0.63)
  waiting for transfers between devices: 137 us -> 0 us
  matrix products: 31.7 us -> 0 us
  Pallas kernels: 225 us -> 252 us
  between operations: 14.2 us -> 0.68 us
    psum x1 -> x0, waiting for transfers between devices: 137 us -> none  [total_over_all(): return lax.psum(x, ('row', 'col'))]
    pallas_call x0 -> x1, Pallas kernels: none -> 52.4 us  [finish(): pl.pallas_call(finish_kernel, out_shape=(jax.ShapeDtypeStruct((rows, cols...]
    dot_general x10 -> x0, matrix products: 31.7 us -> none  [product(): jnp.dot(left, right, precision=lax.Precision.HIGHEST, preferred_element_t...]
    pallas_call x1, Pallas kernels: 225 us -> 199 us  [panels(): pl.pallas_call(panels_kernel, out_shape=(jax.ShapeDtypeStruct((piece, wid...]
    unnamed x31 -> x5, local copies, waits for them, and re-layouts: 8.33 us -> 11.3 us
  transfers between devices with their start and end apart: 1 -> 0, of which waited for: 1 -> 0; matrix products, arithmetic and copies ran while one was open for 1% -> 0% of each run, Pallas kernels for 0% -> 0%
where the time goes in v2:
time: 267 us
  Pallas kernels  252 us (94%)
  local copies, waits for them, and re-layouts  13 us (5%)
    pallas_call x1, Pallas kernels, panels(): pl.pallas_call(panels_kernel, out_shape=(jax.ShapeDtypeStruct((piece, wid...  199 us
    pallas_call x1, Pallas kernels, finish(): pl.pallas_call(finish_kernel, out_shape=(jax.ShapeDtypeStruct((rows, cols...  52.4 us
    unnamed x5, local copies, waits for them, and re-layouts  11.3 us

profile of v2, /device:TPU:0, one launch (start us, length us, event | category | flops | bytes accessed | tf_op | source)
XLA Modules:
  0.0 266.9 jit_solution(9243738880316106589)
XLA Ops:
  0.7 0.8 compare_reduce_fusion
  1.4 0.8 compare_reduce_fusion.1
  2.2 0.9 copy.18.mask2
  3.1 0.9 copy.17.mask1
  3.9 199.3 %panels.1 = (f32[512,512]{1,0:T(8,128)}, f32[512,512]{1,0:T(8,128)}, f32[512,512]{1,0:T(8,128)}, f32[512,512]{1,0:T(8,128)}) custom-call(f32[2048,4096]{1,0:T(8,128)} %trail.1, f32[512,512]{1,0:T(8,128)} %f1.1, f32[512,512]{1,0:T(8,128)} %inv1.3, f32[512,512]{1,0:T(8,128)} %f2.1, f32[512,512]{1,0:T(8,128)} %inv2.3, f32[512,1]{1,0:T(8,128)} %copy.17.mask1, ...), custom_call_target="tpu_custom_call" | custom-call | tf_op jit(solution)/shard_map/panels/pallas_call | solution.py:427
  203.2 52.4 %finish.1 = (f32[512,512]{1,0:T(8,128)}, f32[512,512]{1,0:T(8,128)}, f32[512,512]{1,0:T(8,128)}, f32[512,512]{1,0:T(8,128)}, f32[512,512]{1,0:T(8,128)}) custom-call(f32[512,512]{1,0:T(8,128)} %get-tuple-element.9.y1, f32[512,512]{1,0:T(8,128)} %get-tuple-element.10.y2t, f32[512,512]{1,0:T(8,128)} %get-tuple-element.11.n1, ...), custom_call_target="tpu_custom_call" | custom-call | tf_op jit(solution)/shard_map/finish/pallas_call | solution.py:577
  255.6 2.3 copy.26
  257.9 2.3 copy.27
  260.1 2.3 copy.28
  262.4 2.3 copy.29
  264.7 2.3 copy.30
  (3 shorter events, 0.0 us)

commit v3 on v2

--- a/solution.py
+++ b/solution.py
@@ -63,8 +63,16 @@
     return sum(jnp.where(index == i, v, 0) for i, v in enumerate(table) if v)
 
 
+def row_mask(blocks, piece):
+    first = (lax.axis_index("row") * lax.axis_size("col") + lax.axis_index("col")) * piece
+    listed = blocks[...]
+    rows = first + lax.broadcasted_iota(jnp.int32, (piece, listed.shape[1]), 0)
+    hits = jnp.where(rows // BLK == listed, 1.0, 0.0)
+    return jnp.max(hits, axis=1, keepdims=True)
+
+
 def panels_kernel(
-    trail, f1, inv1, f2, inv2, mask1, mask2, y1_out, y2_out, n1_in, n2_in,
+    trail, f1, inv1, f2, inv2, list1, list2, y1_out, y2_out, n1_in, n2_in,
     n1buf, n2buf, n2h, n2l, out1, out2, rsu, rsd, rsy, y2buf, tbuf, n1h, n1l, cbuf, xbuf,
     f_sem, ag_sem, n2_sem, up_sem, dn_sem, ry_sem, y2_sem, t_sem, c_sem, x_sem,
     s_up, s_dn, s_y, s_root, s_n2, s_ry, s_line, s_c, s_x,
@@ -125,7 +133,7 @@
         cp.start()
     loads[0].wait()
     loads[1].wait()
-    n2_in[...] = (mask2[...] * mm3(out2[0], out2[1])).T
+    n2_in[...] = (row_mask(list2, piece) * mm3(out2[0], out2[1])).T
     own = pltpu.make_async_copy(n2_in, n2buf.at[c], n2_sem.at[0])
     own.start()
 
@@ -138,7 +146,7 @@
 
     loads[2].wait()
     loads[3].wait()
-    n1_in[...] = mask1[...] * mm3(out2[2], out2[3])
+    n1_in[...] = row_mask(list1, piece) * mm3(out2[2], out2[3])
     here = y * 4 + c
     for ch in range(CH):
         part = pl.ds(ch * cr, cr)
@@ -399,7 +407,7 @@
             sent(bit, s_root.at[ch])
 
 
-def panels(trailing, f1, inv1, f2, inv2, mask1, mask2):
+def panels(trailing, f1, inv1, f2, inv2, list1, list2):
     piece, width = f1.shape
     dma = pltpu.SemaphoreType.DMA
     vm = pltpu.VMEM
@@ -438,11 +446,11 @@
             collective_id=0, has_side_effects=True, vmem_limit_bytes=63 * 2**20
         ),
         name="panels",
-    )(trailing, f1, inv1, f2, inv2, mask1, mask2)
+    )(trailing, f1, inv1, f2, inv2, list1, list2)
 
 
 def finish_kernel(
-    y1, y2t, n1, n2t, mask1, mask2, inv1, inv2, f_top,
+    y1, y2t, n1, n2t, list1, list2, inv1, inv2, f_top,
     col1, diag1, col2, cross2, diag2,
     part0, part1, part2, sum0, sum1, sum2, top, top_t, square1, square2,
     acc, got1, got2, got3, got4, recv, send, z_recv, z_send, z_back, z_out,
@@ -532,13 +540,13 @@
 
     def make(m):
         if m == 0:
-            col1[...] = -mask1[...] * y1[...]
+            col1[...] = -row_mask(list1, rows) * y1[...]
             part0[...] = mm3(n1[...].T, col1[...])
         if m == 1:
             part1[...] = mm3(n2t[...], col1[...])
             top[...] = mm3(f_top[...], inv2[...])
         if m == 2:
-            col2[...] = -mask2[...] * (y2t[...].T + mm3(col1[...], top[...]))
+            col2[...] = -row_mask(list2, rows) * (y2t[...].T + mm3(col1[...], top[...]))
             part2[...] = mm3(n2t[...], col2[...])
 
     for step in range(8 + 3):
@@ -568,7 +576,7 @@
                 cp.wait_send()
 
 
-def finish(y1, y2t, n1, n2t, mask1, mask2, inv1, inv2, f_top):
+def finish(y1, y2t, n1, n2t, list1, list2, inv1, inv2, f_top):
     rows, cols = y1.shape
     w = cols // 2
     dma = pltpu.SemaphoreType.DMA
@@ -593,7 +601,23 @@
             collective_id=1, has_side_effects=True, vmem_limit_bytes=60 * 2**20
         ),
         name="finish",
-    )(y1, y2t, n1, n2t, mask1, mask2, inv1, inv2, f_top)
+    )(y1, y2t, n1, n2t, list1, list2, inv1, inv2, f_top)
+
+
+def hand_over_kernel(*refs):
+    for i in range(5):
+        refs[5 + i][...] = refs[i][...]
+
+
+def hand_over(arrays):
+    inv = pl.BlockSpec(memory_space=pltpu.VMEM)
+    return pl.pallas_call(
+        hand_over_kernel,
+        out_shape=tuple(jax.ShapeDtypeStruct(a.shape, a.dtype) for a in arrays),
+        in_specs=[inv] * 5,
+        out_specs=(inv,) * 5,
+        name="hand_over",
+    )(*arrays)
 
 
 def column_panel(normal):
@@ -620,14 +644,15 @@
     structure_two,
 ):
     piece_rows = factor_one.shape[0]
+    if special and piece_rows == factor_one.shape[1]:
+        lists = (structure_one[None, :], structure_two[None, :])
+        sums = panels(trailing, factor_one, inverse_one, factor_two, inverse_two, *lists)
+        return hand_over(finish(*sums, *lists, inverse_one, inverse_two, factor_two_top))
     row_index = lax.axis_index("row")
     col_index = lax.axis_index("col")
     first_row = (row_index * lax.axis_size("col") + col_index) * piece_rows
     mask_one = block_flags(structure_one, first_row, piece_rows)
     mask_two = block_flags(structure_two, first_row, piece_rows)
-    if special and piece_rows == factor_one.shape[1]:
-        sums = panels(trailing, factor_one, inverse_one, factor_two, inverse_two, mask_one, mask_two)
-        return finish(*sums, mask_one, mask_two, inverse_one, inverse_two, factor_two_top)
     normal_one = mask_one * product(factor_one, inverse_one)
     normal_two = mask_two * product(factor_two, inverse_two)
     normal_top = product(factor_two_top, inverse_two)

time: 267 us -> 257 us (0.963)
  local copies, waits for them, and re-layouts: 13 us -> 0 us
  Pallas kernels: 252 us -> 256 us
    unnamed x5 -> x0, local copies, waits for them, and re-layouts: 11.3 us -> none
    pallas_call x0 -> x1, Pallas kernels: none -> 4.91 us  [hand_over(): pl.pallas_call(hand_over_kernel, out_shape=tuple((jax.ShapeDtypeStruct(a....]
where the time goes in v3:
time: 257 us
  Pallas kernels  256 us (100%)
    pallas_call x1, Pallas kernels, panels(): pl.pallas_call(panels_kernel, out_shape=(jax.ShapeDtypeStruct((piece, wid...  199 us
    pallas_call x1, Pallas kernels, finish(): pl.pallas_call(finish_kernel, out_shape=(jax.ShapeDtypeStruct((rows, cols...  52.3 us

profile of v3, /device:TPU:0, one launch (start us, length us, event | category | flops | bytes accessed | tf_op | source)
XLA Modules:
  0.0 256.9 jit_solution(17246828055863319187)
XLA Ops:
  0.6 199.0 %panels.1 = (f32[512,512]{1,0:T(8,128)}, f32[512,512]{1,0:T(8,128)}, f32[512,512]{1,0:T(8,128)}, f32[512,512]{1,0:T(8,128)}) custom-call(f32[2048,4096]{1,0:T(8,128)} %trail.1, f32[512,512]{1,0:T(8,128)} %f1.1, f32[512,512]{1,0:T(8,128)} %inv1.3, f32[512,512]{1,0:T(8,128)} %f2.1, f32[512,512]{1,0:T(8,128)} %inv2.3, s32[1,96]{1,0:T(1,128)} %bitcast.2, ...), custom_call_target="tpu_custom_call" | custom-call | tf_op jit(solution)/shard_map/panels/pallas_call | solution.py:435
  199.6 52.3 %finish.1 = (f32[512,512]{1,0:T(8,128)}, f32[512,512]{1,0:T(8,128)}, f32[512,512]{1,0:T(8,128)}, f32[512,512]{1,0:T(8,128)}, f32[512,512]{1,0:T(8,128)}) custom-call(f32[512,512]{1,0:T(8,128)} %get-tuple-element.14.y1, f32[512,512]{1,0:T(8,128)} %get-tuple-element.15.y2t, f32[512,512]{1,0:T(8,128)} %get-tuple-element.16.n1, ...), custom_call_target="tpu_custom_call" | custom-call | tf_op jit(solution)/shard_map/finish/pallas_call | solution.py:585
  252.0 4.9 %hand_over.1 = (f32[512,512]{1,0:T(8,128)}, f32[512,512]{1,0:T(8,128)}, f32[512,512]{1,0:T(8,128)}, f32[512,512]{1,0:T(8,128)}, f32[512,512]{1,0:T(8,128)}) custom-call(f32[512,512]{1,0:T(8,128)} %get-tuple-element.18.refs_0_, f32[512,512]{1,0:T(8,128)} %get-tuple-element.19.refs_1_, f32[512,512]{1,0:T(8,128)} %get-tuple-element.20.refs_2_, ...), custom_call_target="tpu_custom_call" | custom-call | tf_op jit(solution)/shard_map/hand_over/pallas_call | solution.py:614

commit v4 on v3

--- a/solution.py
+++ b/solution.py
@@ -11,17 +11,20 @@
 MESH = pl.DeviceIdType.MESH
 CH = 8
 AG_LAG = 1
-RS_LAG = 4
+RS_LAG = 5
 RS0 = 10
-Y0 = 9
-Y_RATE = 2
-ROOT_RATE = 2
-AG_O, AG_T = (0, 0, 0, 0, 1), (1, 0, 2, 3, 0)
-RS_O, RS_T = (1, 0, 0, 0, 0), (0, 3, 2, 1, 0)
-B_O, B_T = (1, 1, 0, 1, 0, 1, 0, 0), (0, 3, 3, 2, 2, 1, 1, 0)
-A_O, A_T = (0, 0, 1, 0, 0, 1, 1, 1), (1, 0, 1, 2, 3, 2, 0, 3)
+Y0 = 16
+NEAR0 = 16
+ROOT0 = 41
+X_TICK = 8
+AG_O, AG_T = (0, 0, 0, 0, 1, 1), (1, 0, 2, 3, 0, 1)
+RS_O, RS_T = (1, 0, 0, 0, 0), (0, 3, 2, 0, 1)
+B_O, B_T = (1, 1, 1, 0, 1, 0, 0, 0), (0, 1, 3, 3, 2, 2, 1, 0)
+A_O, A_T = (0, 0, 0, 0, 1, 1, 1, 1), (1, 0, 2, 3, 0, 2, 3, 1)
 Y_T = (3, 2, 1)
-A_TICK = (16, 17, 19, 20, 21, 22, 27, 28, 35, 36, 37, 38, 43, 44, 45, 46)
+QR = CH // 2
+AG_N = 2 * len(AG_T) * QR
+A_TICK = (20, 21, 22, 23, 24, 25, 26, 27, 31, 35, 39, 43, 47, 48, 49, 51)
 F32 = jnp.float32
 BF16 = jnp.bfloat16
 
@@ -73,20 +76,22 @@
 
 def panels_kernel(
     trail, f1, inv1, f2, inv2, list1, list2, y1_out, y2_out, n1_in, n2_in,
-    n1buf, n2buf, n2h, n2l, out1, out2, rsu, rsd, rsy, y2buf, tbuf, n1h, n1l, cbuf, xbuf,
-    f_sem, ag_sem, n2_sem, up_sem, dn_sem, ry_sem, y2_sem, t_sem, c_sem, x_sem,
+    n1buf, n2buf, n2h, n2l, out1, out2, rsu, rsd, rsy, rsn, y2buf, tbuf, n1h, n1l, cbuf, xbuf,
+    f_sem, near_sem, ag_sem, n2_sem, up_sem, dn_sem, ry_sem, y2_sem, t_sem, c_sem, x_sem,
     s_up, s_dn, s_y, s_root, s_n2, s_ry, s_line, s_c, s_x,
 ):
     r, c = lax.axis_index("row"), lax.axis_index("col")
     z, y, x, k = r // 2, r % 2, c // 2, c % 2
     piece = n1_in.shape[0]
-    cr = piece // CH
+    width = n1_in.shape[1]
+    cr, gw = piece // QR, width // 2
     wr = n2_in.shape[0] // CH
     ypart = (r + 1 - 2 * y, c)
     cpart = (r, flip(c, 1))
     xpart = (r, flip(c, 2))
     above = (lax.rem(r + 2, 8), c)
     below = (lax.rem(r + 6, 8), c)
+    near = jnp.where((z // 2 == x) & (z != c), 1, 0)
     dist = jnp.where(z > c, z - c, c - z)
 
     def remote(src, dst, send, recv, to):
@@ -94,6 +99,12 @@
             src_ref=src, dst_ref=dst, send_sem=send, recv_sem=recv, device_id=to, device_id_type=MESH
         )
 
+    def cols_of(g):
+        return pl.ds(pl.multiple_of(g * gw, gw), gw)
+
+    def chunk_of(ch):
+        return pl.ds(pl.multiple_of((ch % QR) * cr, cr), cr), cols_of(ch // QR)
+
     def arrived(ref, sem):
         pltpu.make_async_copy(ref, ref, sem).wait()
 
@@ -110,13 +121,12 @@
         pl.semaphore_signal(bar, inc=1, device_id=below, device_id_type=MESH)
 
     def tile_of(u):
-        isa = u // 16
-        v = u % 16
-        hb, ha = (x + v // 8) % 2, v % 2
-        pb, pa = v % 8, v // 2
+        isa = jnp.where(u >= 16, 1, 0)
+        w = (u - 16) * isa
+        pb, pa = u % 8, (w // 2) % 8
         t = isa * pick(A_T, pa) + (1 - isa) * pick(B_T, pb)
         o = isa * pick(A_O, pa) + (1 - isa) * pick(B_O, pb)
-        h = isa * ha + (1 - isa) * hb
+        h = isa * (w % 2) + (1 - isa) * ((x + u // 8) % 2)
         return ((y + o) % 2) * 4 + flip(c, t), h, t, o
 
     half = 2 * piece
@@ -149,15 +159,15 @@
     n1_in[...] = row_mask(list1, piece) * mm3(out2[2], out2[3])
     here = y * 4 + c
     for ch in range(CH):
-        part = pl.ds(ch * cr, cr)
+        part = chunk_of(ch)
 
         @pl.when(c == z)
         def _():
-            pltpu.make_async_copy(n1_in.at[part], n1buf.at[here, part], ag_sem.at[here, ch]).start()
+            pltpu.make_async_copy(n1_in.at[part], n1buf.at[(here, *part)], ag_sem.at[here, ch]).start()
 
         @pl.when(c != z)
         def _():
-            remote(n1_in.at[part], n1buf.at[here, part], s_root.at[ch], ag_sem.at[here, ch], (r, z)).start()
+            remote(n1_in.at[part], n1buf.at[(here, *part)], s_root.at[ch], ag_sem.at[here, ch], (r, z)).start()
 
     own.wait()
     arrived(n2buf.at[flip(c, 1)], n2_sem.at[1])
@@ -165,12 +175,17 @@
         q = flip(c, t)
         n2h[q], n2l[q] = split(n2buf[q])
 
+    def ag_of(n):
+        g, s, i = n // (len(AG_T) * QR), (n // QR) % len(AG_T), n % QR
+        return pick(AG_O, s), pick(AG_T, s), g * QR + i
+
+    def goes_y(o, t):
+        return (o == 0) & ((t > 1) | (z == c))
+
     def ag_step(n):
-        s, ch = n // CH, n % CH
-        o, t = pick(AG_O, s), pick(AG_T, s)
+        o, t, ch = ag_of(n)
         j = ((y + o) % 2) * 4 + flip(c, t)
-        part = pl.ds(pl.multiple_of(ch * cr, cr), cr)
-        chunk = n1buf.at[j, part]
+        chunk = n1buf.at[(j, *chunk_of(ch))]
         arrived(chunk, ag_sem.at[j, ch])
 
         @pl.when((z >= c) & (z < 3))
@@ -181,7 +196,7 @@
         def _():
             remote(chunk, chunk, s_dn.at[n], ag_sem.at[j, ch], below).start()
 
-        @pl.when((o == 0) & ((t > 0) | (z == c)))
+        @pl.when(goes_y(o, t))
         def _():
             remote(chunk, chunk, s_y.at[t, ch], ag_sem.at[j, ch], ypart).start()
 
@@ -202,7 +217,7 @@
             arrived(rsd.at[s, part], dn_sem.at[n])
             chunk[...] += rsd[s, part]
 
-        @pl.when((o == 0) & ((t > 0) | (z == c)))
+        @pl.when((o == 0) & ((t > 1) | (z == c) | ((t == 1) & (near == 0))))
         def _():
             arrived(rsy.at[t, part], ry_sem.at[t, ch])
             chunk[...] += rsy[t, part]
@@ -251,61 +266,79 @@
         t, ch = pick(Y_T, q // CH), q % CH
         part = pl.ds(pl.multiple_of(ch * wr, wr), wr)
         j = ((y + 1) % 2) * 4 + flip(c, t)
-        remote(out2.at[j, part], rsy.at[t, part], s_ry.at[t, ch], ry_sem.at[t, ch], ypart).start()
-
-    def turn_a(u):
-        j, h, t, o = tile_of(u)
-
-        @pl.when((h == 0) & (o == 1) & (t >= 1))
-        def _():
-            for ch in range(CH):
-                arrived(n1buf.at[j, pl.ds(ch * cr, cr)], ag_sem.at[j, ch])
-
-        @pl.when(h == 0)
-        def _():
-            n1h[...], n1l[...] = split(n1buf[j])
-
-        fetch(u).wait()
-
-        @pl.when(u < 31)
-        def _():
-            fetch(u + 1).start()
+
+        @pl.when((t > 1) | ((near == 0) & (z != c)))
+        def _():
+            remote(out2.at[j, part], rsy.at[t, part], s_ry.at[t, ch], ry_sem.at[t, ch], ypart).start()
+
+    j_near = ((y + 1) % 2) * 4 + flip(c, 1)
+
+    def near_step(ch):
+        part = pl.ds(pl.multiple_of(ch * wr, wr), wr)
+        remote(out2.at[j_near, part], rsn.at[part], s_ry.at[1, ch], near_sem.at[ch], (lax.rem(r + jnp.where(z < c, 2, 6), 8), c)).start()
+
+    def root_step(ch):
+        part = pl.ds(pl.multiple_of(ch * wr, wr), wr)
+        arrived(rsn.at[part], near_sem.at[ch])
+        out2[j_near, part] += rsn[part]
+        remote(out2.at[j_near, part], rsy.at[1, part], s_ry.at[1, ch], ry_sem.at[1, ch], ypart).start()
+
+    def turn_a(turn):
+        g = turn // 8
+        cols = cols_of(g)
+        j, _, t, o = tile_of(16 + 2 * turn)
+
+        @pl.when((o == 1) & (t >= 2))
+        def _():
+            for i in range(QR):
+                ch = g * QR + i
+                arrived(n1buf.at[(j, *chunk_of(ch))], ag_sem.at[j, ch])
+
+        n1h[...], n1l[...] = split(n1buf[j, :, cols])
 
         @pl.loop(0, 2)
-        def _(i):
-            rows = pl.ds(pl.multiple_of(i * piece, piece), piece)
-            th, tl = split(tbuf[u % 2, rows])
-            add = mm(th, n1h[...]) + (mm(th, n1l[...]) + mm(tl, n1h[...]))
-            q = 2 * h + i
-
-            @pl.when(u < 18)
+        def _(h):
+            u = 16 + 2 * turn + h
+            fetch(u).wait()
+
+            @pl.when(u < 47)
             def _():
-                out1[q] = add
-
-            @pl.when(u >= 18)
-            def _():
-                out1[q] += add
+                fetch(u + 1).start()
+
+            @pl.loop(0, 2)
+            def _(i):
+                rows = pl.ds(pl.multiple_of(i * piece, piece), piece)
+                th, tl = split(tbuf[u % 2, rows])
+                add = mm(th, n1h[...]) + (mm(th, n1l[...]) + mm(tl, n1h[...]))
+                q = 2 * h + i
+
+                @pl.when(turn % 8 == 0)
+                def _():
+                    out1[q, :, cols] = add
+
+                @pl.when(turn % 8 > 0)
+                def _():
+                    out1[q, :, cols] += add
 
     qx = flip(c, 2)
-    end_a = A_TICK[15] + 1
     ag_first = AG_LAG * dist
-    ag_rate = jnp.where(z == c, ROOT_RATE, 1)
     rs_first = RS0 + RS_LAG * jnp.where(z > c, 3 - z, jnp.where(z < c, z, jnp.where(c < 2, 3 - c, c)))
 
-    def core_copy(i):
+    def core_copy(g, i):
         to = flip(c, 1 + 2 * (1 - i))
-        return remote(out1.at[to], cbuf.at[i], s_c.at[i], c_sem.at[i], cpart)
-
-    x_copy = remote(out1.at[qx], xbuf, s_x.at[0], x_sem.at[0], xpart)
+        cols = cols_of(g)
+        return remote(out1.at[to, :, cols], cbuf.at[i, :, cols], s_c.at[g, i], c_sem.at[g, i], cpart)
+
+    def x_copy(g):
+        cols = cols_of(g)
+        return remote(out1.at[qx, :, cols], xbuf.at[:, cols], s_x.at[g], x_sem.at[g], xpart)
 
     def tick(step, carry):
-        @pl.loop(0, ag_rate)
-        def _(i):
-            n = (step - ag_first) * ag_rate + i
-
-            @pl.when((n >= 0) & (n < 5 * CH))
-            def _():
-                ag_step(n)
+        n = step - ag_first
+
+        @pl.when((n >= 0) & (n < AG_N))
+        def _():
+            ag_step(n)
 
         m = step - rs_first
 
@@ -313,7 +346,7 @@
         def _():
             rs_step(m)
 
-        @pl.when(step == 8)
+        @pl.when(step == X_TICK)
         def _():
             got = flip(c, 2)
             arrived(n2buf.at[got], n2_sem.at[2])
@@ -328,36 +361,53 @@
         def _():
             turn_b(step)
 
-        for i in range(Y_RATE):
-            q = (step - Y0) * Y_RATE + i
-
-            @pl.when((q >= 0) & (q < 3 * CH))
+        for i in range(2):
+            e = (step - NEAR0) * 2 + i
+
+            @pl.when((near == 1) & (e >= 0) & (e < CH))
             def _():
-                y_step(q)
+                near_step(e)
+
+        e = step - ROOT0
+
+        @pl.when((z == c) & (e >= 0) & (e < CH))
+        def _():
+            root_step(e)
+
+        q = step - Y0
+
+        @pl.when((q >= 0) & (q < 3 * CH))
+        def _():
+            y_step(q)
 
         @pl.when(sum(jnp.where(step == a, 1, 0) for a in A_TICK) > 0)
         def _():
-            turn_a(15 + sum(jnp.where(step >= a, 1, 0) for a in A_TICK))
-
-        @pl.when(step == end_a)
-        def _():
-            core_copy(0).start()
-            core_copy(1).start()
-
-        @pl.when(step == end_a + 1)
-        def _():
-            core_copy(0).wait_recv()
-            out1[qx] += cbuf[0]
-            x_copy.start()
-            core_copy(1).wait_recv()
-            out1[c] += cbuf[1]
+            turn_a(sum(jnp.where(step >= a, 1, 0) for a in A_TICK) - 1)
+
+        for g in range(2):
+            end_a = A_TICK[8 * g + 7] + 1
+
+            @pl.when(step == end_a)
+            def _():
+                core_copy(g, 0).start()
+                core_copy(g, 1).start()
+
+            @pl.when(step == end_a + 1)
+            def _():
+                cols = cols_of(g)
+                core_copy(g, 0).wait_recv()
+                out1[qx, :, cols] += cbuf[0, :, cols]
+                x_copy(g).start()
+                core_copy(g, 1).wait_recv()
+                out1[c, :, cols] += cbuf[1, :, cols]
 
         return carry
 
-    last_tick = RS0 + 3 * RS_LAG + 5 * CH
-    lax.fori_loop(0, max(last_tick, end_a + 2), tick, 0)
-
-    x_copy.wait_recv()
+    last_tick = max(RS0 + 3 * RS_LAG + 5 * CH, AG_N + 3 * AG_LAG, A_TICK[15] + 3, Y0 + 3 * CH)
+    lax.fori_loop(0, last_tick, tick, 0)
+
+    for g in range(2):
+        x_copy(g).wait_recv()
     y1_out[...] = out1[c] + xbuf[...]
     for ch in range(CH):
         part = pl.ds(ch * wr, wr)
@@ -370,29 +420,32 @@
     whole = n2buf.at[0]
     for i in range(3):
         sent(whole, s_n2.at[i])
-    for i in range(2):
-        sent(cbuf.at[0], s_c.at[i])
-    sent(xbuf, s_x.at[0])
-    bit = n1buf.at[0, pl.ds(0, cr)]
+    for g in range(2):
+        for i in range(2):
+            core_copy(g, i).wait_send()
+        x_copy(g).wait_send()
+    bit = n1buf.at[(0, *chunk_of(0))]
     wbit = out2.at[0, pl.ds(0, wr)]
+
+    @pl.loop(0, AG_N)
+    def _(n):
+        o, t, ch = ag_of(n)
+
+        @pl.when((z >= c) & (z < 3))
+        def _():
+            sent(bit, s_up.at[n])
+
+        @pl.when((z <= c) & (z > 0))
+        def _():
+            sent(bit, s_dn.at[n])
+
+        @pl.when(goes_y(o, t))
+        def _():
+            sent(bit, s_y.at[t, ch])
 
     @pl.loop(0, 5 * CH)
     def _(n):
         s, ch = n // CH, n % CH
-
-        @pl.when((z >= c) & (z < 3))
-        def _():
-            sent(bit, s_up.at[n])
-
-        @pl.when((z <= c) & (z > 0))
-        def _():
-            sent(bit, s_dn.at[n])
-
-        o, t = pick(AG_O, s), pick(AG_T, s)
-
-        @pl.when((o == 0) & ((t > 0) | (z == c)))
-        def _():
-            sent(bit, s_y.at[t, ch])
 
         @pl.when((z != c) | (pick(RS_O, s) == 1) | (pick(RS_T, s) > 0))
         def _():
@@ -422,13 +475,14 @@
         vm((5, width, piece), F32),
         vm((4, width, piece), F32),
         vm((width, piece), F32),
+        vm((width, piece), F32),
         vm((2, 2 * piece, piece), F32),
-        vm((piece, width), BF16),
-        vm((piece, width), BF16),
+        vm((piece, width // 2), BF16),
+        vm((piece, width // 2), BF16),
         vm((2, piece, width), F32),
         vm((piece, width), F32),
-        dma((4,)), dma((8, CH)), dma((4,)), dma((5 * CH,)), dma((5 * CH,)), dma((4, CH)), dma((CH,)), dma((2,)), dma((2,)), dma((1,)),
-        dma((5 * CH,)), dma((5 * CH,)), dma((4, CH)), dma((CH,)), dma((3,)), dma((4, CH)), dma((5 * CH,)), dma((2,)), dma((1,)),
+        dma((4,)), dma((CH,)), dma((8, CH)), dma((4,)), dma((5 * CH,)), dma((5 * CH,)), dma((4, CH)), dma((CH,)), dma((2,)), dma((2, 2)), dma((2,)),
+        dma((AG_N,)), dma((AG_N,)), dma((4, CH)), dma((CH,)), dma((3,)), dma((4, CH)), dma((5 * CH,)), dma((2, 2)), dma((2,)),
     ]
     anyspace = pl.BlockSpec(memory_space=pl.ANY)
     inv = pl.BlockSpec(memory_space=pltpu.VMEM)

time: 257 us -> 253 us (0.984)
  Pallas kernels: 256 us -> 252 us
    pallas_call x1, Pallas kernels: 199 us -> 193 us  [panels(): pl.pallas_call(panels_kernel, out_shape=(jax.ShapeDtypeStruct((piece, wid...]
where the time goes in v4:
time: 253 us; the launch traced here: 252 us
  Pallas kernels  252 us (100%)
    pallas_call x1, Pallas kernels, panels(): pl.pallas_call(panels_kernel, out_shape=(jax.ShapeDtypeStruct((piece, wid...  193 us
    pallas_call x1, Pallas kernels, finish(): pl.pallas_call(finish_kernel, out_shape=(jax.ShapeDtypeStruct((rows, cols...  53.3 us

profile of v4, /device:TPU:0, one launch (start us, length us, event | category | flops | bytes accessed | tf_op | source)
XLA Modules:
  0.0 252.2 jit_solution(9354831707369746730)
XLA Ops:
  0.6 193.3 %panels.1 = (f32[512,512]{1,0:T(8,128)}, f32[512,512]{1,0:T(8,128)}, f32[512,512]{1,0:T(8,128)}, f32[512,512]{1,0:T(8,128)}) custom-call(f32[2048,4096]{1,0:T(8,128)} %trail.1, f32[512,512]{1,0:T(8,128)} %f1.1, f32[512,512]{1,0:T(8,128)} %inv1.3, f32[512,512]{1,0:T(8,128)} %f2.1, f32[512,512]{1,0:T(8,128)} %inv2.3, s32[1,96]{1,0:T(1,128)} %bitcast.2, ...), custom_call_target="tpu_custom_call" | custom-call | tf_op jit(solution)/shard_map/panels/pallas_call | solution.py:489
  193.9 53.3 %finish.1 = (f32[512,512]{1,0:T(8,128)}, f32[512,512]{1,0:T(8,128)}, f32[512,512]{1,0:T(8,128)}, f32[512,512]{1,0:T(8,128)}, f32[512,512]{1,0:T(8,128)}) custom-call(f32[512,512]{1,0:T(8,128)} %get-tuple-element.14.y1, f32[512,512]{1,0:T(8,128)} %get-tuple-element.15.y2t, f32[512,512]{1,0:T(8,128)} %get-tuple-element.16.n1, ...), custom_call_target="tpu_custom_call" | custom-call | tf_op jit(solution)/shard_map/finish/pallas_call | solution.py:639
  247.3 4.9 %hand_over.1 = (f32[512,512]{1,0:T(8,128)}, f32[512,512]{1,0:T(8,128)}, f32[512,512]{1,0:T(8,128)}, f32[512,512]{1,0:T(8,128)}, f32[512,512]{1,0:T(8,128)}) custom-call(f32[512,512]{1,0:T(8,128)} %get-tuple-element.18.refs_0_, f32[512,512]{1,0:T(8,128)} %get-tuple-element.19.refs_1_, f32[512,512]{1,0:T(8,128)} %get-tuple-element.20.refs_2_, ...), custom_call_target="tpu_custom_call" | custom-call | tf_op jit(solution)/shard_map/hand_over/pallas_call | solution.py:668

commit v5 on v4

--- a/solution.py
+++ b/solution.py
@@ -143,20 +143,27 @@
         cp.start()
     loads[0].wait()
     loads[1].wait()
-    n2_in[...] = (row_mask(list2, piece) * mm3(out2[0], out2[1])).T
-    own = pltpu.make_async_copy(n2_in, n2buf.at[c], n2_sem.at[0])
-    own.start()
+    cut = width // 2
+    left, right = pl.ds(0, cut), pl.ds(cut, cut)
+    listed = row_mask(list2, piece)
+
+    def send_half(rows):
+        remote(n2_in.at[rows], n2buf.at[c, rows], s_n2.at[0], n2_sem.at[2], xpart).start()
+        remote(n2_in.at[rows], n2buf.at[c, rows], s_n2.at[1], n2_sem.at[1], cpart).start()
+        pltpu.make_async_copy(n2_in.at[rows], n2buf.at[c, rows], n2_sem.at[0]).start()
+
+    n2_in[right] = (listed * mm3(out2[0, :, right], out2[1, right, right])).T
 
     pl.semaphore_wait(bar, 4 + (z + 2) // 3 + (5 - z) // 3)
-
-    to_x = remote(n2_in, n2buf.at[c], s_n2.at[0], n2_sem.at[2], xpart)
-    to_x.start()
-    to_c = remote(n2_in, n2buf.at[c], s_n2.at[1], n2_sem.at[1], cpart)
-    to_c.start()
+    send_half(right)
+    n2_in[left] = (listed * mm3(out2[0], out2[1, :, left])).T
+    send_half(left)
 
     loads[2].wait()
     loads[3].wait()
-    n1_in[...] = row_mask(list1, piece) * mm3(out2[2], out2[3])
+    listed = row_mask(list1, piece)
+    n1_in[:, left] = listed * mm3(out2[2], out2[3, :, left])
+    n1_in[:, right] = listed * mm3(out2[2, :, right], out2[3, right, right])
     here = y * 4 + c
     for ch in range(CH):
         part = chunk_of(ch)
@@ -169,7 +176,7 @@
         def _():
             remote(n1_in.at[part], n1buf.at[(here, *part)], s_root.at[ch], ag_sem.at[here, ch], (r, z)).start()
 
-    own.wait()
+    arrived(n2buf.at[c], n2_sem.at[0])
     arrived(n2buf.at[flip(c, 1)], n2_sem.at[1])
     for t in range(2):
         q = flip(c, t)
@@ -515,14 +522,15 @@
     ypart = (r + 1 - 2 * y, c)
     cpart = (r, flip(c, 1))
     xpart = (r, flip(c, 2))
-    rows, cols = parts[0].shape
-    h1, h2, h3, h4 = rows // 2, rows // 4, rows // 8, rows // 32
-    side = [pl.ds(0, cols // 2), pl.ds(cols // 2, cols // 2)]
+    rows, cols = part1.shape
+    half, quarter = rows // 2, rows // 4
+    zw = cols // 4
     first, second = (x, y), (y, x)
     one, two = (xpart, ypart), (ypart, xpart)
-    base = k * h1
-    at1 = [first[i] * h2 for i in (0, 1)]
-    at2 = [at1[i] + second[i] * h3 for i in (0, 1)]
+    h1, h2, h3 = ([parts[m].shape[0] // d for m in range(3)] for d in (2, 8, 16))
+    base = [k * h1[m] for m in range(3)]
+    at1 = [[i * (h1[m] // 2) + first[i] * h2[m] for i in (0, 1)] for m in range(3)]
+    at2 = [[at1[m][i] + second[i] * h3[m] for i in (0, 1)] for m in range(3)]
     line = [(lax.rem(r + 2 * d, 8), c) for d in (1, 2, 3)]
 
     def remote(src, dst, s_sem, r_sem, to):
@@ -531,7 +539,10 @@
         )
 
     def span(start, size):
-        return pl.ds(pl.multiple_of(start, size), size)
+        return pl.ds(pl.multiple_of(start, 8), size)
+
+    def side(zz):
+        return pl.ds(pl.multiple_of(zz * zw, zw), zw)
 
     bar = pltpu.get_barrier_semaphore()
     for to in [ypart, cpart, xpart] + line:
@@ -540,76 +551,95 @@
 
     def copies(m, stage):
         if stage == 0:
-            return [remote(parts[m].at[span((1 - k) * h1, h1)], got1.at[m], send.at[m, 0, 0], recv.at[m, 0, 0], cpart)]
+            there = parts[m].at[span((1 - k) * h1[m], h1[m])]
+            return [remote(there, got1.at[m, span(0, h1[m])], send.at[m, 0, 0], recv.at[m, 0, 0], cpart)]
         if stage == 1:
             return [
-                remote(acc.at[m, span((1 - first[i]) * h2, h2), side[i]], got2.at[m, i], send.at[m, 1, i], recv.at[m, 1, i], one[i])
+                remote(
+                    acc.at[m, span(i * (h1[m] // 2) + (1 - first[i]) * h2[m], h2[m])],
+                    got2.at[m, i, span(0, h2[m])], send.at[m, 1, i], recv.at[m, 1, i], one[i],
+                )
                 for i in (0, 1)
             ]
         if stage == 2:
             return [
                 remote(
-                    acc.at[m, span(at1[i] + (1 - second[i]) * h3, h3), side[i]],
-                    got3.at[m, i], send.at[m, 2, i], recv.at[m, 2, i], two[i],
+                    acc.at[m, span(at1[m][i] + (1 - second[i]) * h3[m], h3[m])],
+                    got3.at[m, i, span(0, h3[m])], send.at[m, 2, i], recv.at[m, 2, i], two[i],
                 )
                 for i in (0, 1)
             ]
         if stage == 3:
             return [
                 remote(
-                    acc.at[m, span(at2[i] + lax.rem(z + d, 4) * h4, h4), side[i]],
-                    got4.at[m, d - 1, i], z_send.at[m, d - 1, i], z_recv.at[m, d - 1, i], line[d - 1],
+                    acc.at[m, span(at2[m][i], h3[m]), side(lax.rem(z + d, 4))],
+                    got4.at[m, d - 1, i, span(0, h3[m])], z_send.at[m, d - 1, i], z_recv.at[m, d - 1, i], line[d - 1],
                 )
                 for d in (1, 2, 3)
                 for i in (0, 1)
             ]
         if stage == 4:
-            places = [outs[m].at[span(base + at2[i] + z * h4, h4), side[i]] for i in (0, 1)]
+            places = [outs[m].at[span(base[m] + at2[m][i], h3[m]), side(z)] for i in (0, 1)]
             return [
                 remote(places[i], places[i], z_out.at[m, d - 1, i], z_back.at[m, d - 1, i], line[d - 1])
                 for d in (1, 2, 3)
                 for i in (0, 1)
             ]
         if stage == 7:
-            place = outs[m].at[span(base, h1)]
+            place = outs[m].at[span(base[m], h1[m])]
             return [remote(place, place, send.at[m, 5, 0], recv.at[m, 5, 0], cpart)]
         to = (two, one)[stage - 5]
-        size, at = ((h3, at2), (h2, at1))[stage - 5]
-        places = [outs[m].at[span(base + at[i], size), side[i]] for i in (0, 1)]
+        size, at = ((h3[m], at2[m]), (h2[m], at1[m]))[stage - 5]
+        places = [outs[m].at[span(base[m] + at[i], size)] for i in (0, 1)]
         return [remote(places[i], places[i], send.at[m, stage - 2, i], recv.at[m, stage - 2, i], to[i]) for i in (0, 1)]
 
     def take(m, stage):
         for cp in copies(m, stage):
             cp.wait_recv()
         if stage == 0:
-            acc[m] = parts[m][span(base, h1)] + got1[m]
+            acc[m, span(0, h1[m])] = parts[m][span(base[m], h1[m])] + got1[m, span(0, h1[m])]
         for i in (0, 1):
             if stage == 1:
-                acc[m, span(at1[i], h2), side[i]] += got2[m, i]
+                acc[m, span(at1[m][i], h2[m])] += got2[m, i, span(0, h2[m])]
             if stage == 2:
-                acc[m, span(at2[i], h3), side[i]] += got3[m, i]
+                acc[m, span(at2[m][i], h3[m])] += got3[m, i, span(0, h3[m])]
             if stage == 3:
-                mine = acc[m, span(at2[i] + z * h4, h4), side[i]] + got4[m, 0, i] + (got4[m, 1, i] + got4[m, 2, i])
-                outs[m][span(base + at2[i] + z * h4, h4), side[i]] = mine
+                got = [got4[m, d, i, span(0, h3[m])] for d in range(3)]
+                mine = acc[m, span(at2[m][i], h3[m]), side(z)] + got[0] + (got[1] + got[2])
+                outs[m][span(base[m] + at2[m][i], h3[m]), side(z)] = mine
+
+    def pack(part, left, right):
+        part[0:half] = mm3(left[0:half], right)
+        last = mm3(left[half:rows], right[:, half:cols])
+        part[half : half + quarter, 0:half] = last[0:quarter]
+        part[half : half + quarter, half:cols] = last[quarter:half]
+
+    def minus(out, value, total):
+        out[0:half] = value[0:half] - total[0:half]
+        out[half:rows, 0:half] = value[half:rows, 0:half] - total[0:half, half:cols].T
+        out[half : half + quarter, half:cols] = value[half : half + quarter, half:cols] - total[half : half + quarter, 0:half]
+        out[half + quarter : rows, half:cols] = value[half + quarter : rows, half:cols] - total[half : half + quarter, half:cols]
 
     def make(m):
         if m == 0:
             col1[...] = -row_mask(list1, rows) * y1[...]
-            part0[...] = mm3(n1[...].T, col1[...])
+            pack(part0, n1[...].T, col1[...])
         if m == 1:
             part1[...] = mm3(n2t[...], col1[...])
-            top[...] = mm3(f_top[...], inv2[...])
         if m == 2:
-            col2[...] = -row_mask(list2, rows) * (y2t[...].T + mm3(col1[...], top[...]))
-            part2[...] = mm3(n2t[...], col2[...])
+            col2[...] = -row_mask(list2, rows) * y2t[...].T
+            pack(part2, n2t[...], col2[...])
 
     for step in range(8 + 3):
         if step == 3:
+            top[...] = mm3(f_top[...], inv2[...])
             square1[...] = mm3(inv1[...].T, inv1[...])
         if step == 4:
             square2[...] = mm3(inv2[...].T, inv2[...])
         if step == 5:
             top_t[...] = top[...].T
+        if step == 6:
+            col2[...] -= row_mask(list2, rows) * mm3(col1[...], top[...])
         for m in range(3):
             stage = step - m
             if stage == 0:
@@ -620,10 +650,10 @@
                 for cp in copies(m, stage):
                     cp.start()
         if step == 9:
-            diag1[...] = square1[...] - sum0[...]
+            minus(diag1, square1, sum0)
             cross2[...] = -(mm3(diag1[...], top[...]) + sum1[...].T)
-            square2[...] -= mm3(top_t[...], cross2[...])
-    diag2[...] = square2[...] - sum2[...]
+            square2[...] += mm3(sum1[...], top[...]) - mm3(top_t[...], cross2[...])
+    minus(diag2, square2, sum2)
     for m in range(3):
         for stage in range(8):
             for cp in copies(m, stage):
@@ -632,7 +662,6 @@
 
 def finish(y1, y2t, n1, n2t, list1, list2, inv1, inv2, f_top):
     rows, cols = y1.shape
-    w = cols // 2
     dma = pltpu.SemaphoreType.DMA
     vm = pltpu.VMEM
     inv = pl.BlockSpec(memory_space=pltpu.VMEM)
@@ -642,12 +671,14 @@
         in_specs=[inv] * 9,
         out_specs=(inv,) * 5,
         scratch_shapes=[
-            *[vm((rows, cols), F32)] * 10,
+            vm((3 * rows // 4, cols), F32), vm((rows, cols), F32), vm((3 * rows // 4, cols), F32),
+            vm((3 * rows // 4, cols), F32), vm((rows, cols), F32), vm((3 * rows // 4, cols), F32),
+            *[vm((rows, cols), F32)] * 4,
             vm((3, rows // 2, cols), F32),
             vm((3, rows // 2, cols), F32),
-            vm((3, 2, rows // 4, w), F32),
-            vm((3, 2, rows // 8, w), F32),
-            vm((3, 3, 2, rows // 32, w), F32),
+            vm((3, 2, rows // 8, cols), F32),
+            vm((3, 2, rows // 16, cols), F32),
+            vm((3, 3, 2, rows // 16, cols // 4), F32),
             dma((3, 6, 2)), dma((3, 6, 2)),
             dma((3, 3, 2)), dma((3, 3, 2)), dma((3, 3, 2)), dma((3, 3, 2)),
         ],

time: 253 us -> 250 us (0.988)
  Pallas kernels: 252 us -> 249 us
where the time goes in v5:
time: 250 us
  Pallas kernels  249 us (100%)
    pallas_call x1, Pallas kernels, panels(): pl.pallas_call(panels_kernel, out_shape=(jax.ShapeDtypeStruct((piece, wid...  193 us
    pallas_call x1, Pallas kernels, finish(): pl.pallas_call(finish_kernel, out_shape=(jax.ShapeDtypeStruct((rows, cols...  51.1 us

profile of v5, /device:TPU:0, one launch (start us, length us, event | category | flops | bytes accessed | tf_op | source)
XLA Modules:
  0.0 249.7 jit_solution(437358845449783418)
XLA Ops:
  0.6 193.0 %panels.1 = (f32[512,512]{1,0:T(8,128)}, f32[512,512]{1,0:T(8,128)}, f32[512,512]{1,0:T(8,128)}, f32[512,512]{1,0:T(8,128)}) custom-call(f32[2048,4096]{1,0:T(8,128)} %trail.1, f32[512,512]{1,0:T(8,128)} %f1.1, f32[512,512]{1,0:T(8,128)} %inv1.3, f32[512,512]{1,0:T(8,128)} %f2.1, f32[512,512]{1,0:T(8,128)} %inv2.3, s32[1,96]{1,0:T(1,128)} %bitcast.2, ...), custom_call_target="tpu_custom_call" | custom-call | tf_op jit(solution)/shard_map/panels/pallas_call | solution.py:496
  193.7 51.1 %finish.1 = (f32[512,512]{1,0:T(8,128)}, f32[512,512]{1,0:T(8,128)}, f32[512,512]{1,0:T(8,128)}, f32[512,512]{1,0:T(8,128)}, f32[512,512]{1,0:T(8,128)}) custom-call(f32[512,512]{1,0:T(8,128)} %get-tuple-element.14.y1, f32[512,512]{1,0:T(8,128)} %get-tuple-element.15.y2t, f32[512,512]{1,0:T(8,128)} %get-tuple-element.16.n1, ...), custom_call_target="tpu_custom_call" | custom-call | tf_op jit(solution)/shard_map/finish/pallas_call | solution.py:668
  244.8 4.9 %hand_over.1 = (f32[512,512]{1,0:T(8,128)}, f32[512,512]{1,0:T(8,128)}, f32[512,512]{1,0:T(8,128)}, f32[512,512]{1,0:T(8,128)}, f32[512,512]{1,0:T(8,128)}) custom-call(f32[512,512]{1,0:T(8,128)} %get-tuple-element.18.refs_0_, f32[512,512]{1,0:T(8,128)} %get-tuple-element.19.refs_1_, f32[512,512]{1,0:T(8,128)} %get-tuple-element.20.refs_2_, ...), custom_call_target="tpu_custom_call" | custom-call | tf_op jit(solution)/shard_map/hand_over/pallas_call | solution.py:699

commit v6 on v5

--- a/solution.py
+++ b/solution.py
@@ -13,17 +13,18 @@
 AG_LAG = 1
 RS_LAG = 5
 RS0 = 10
-Y0 = 16
-NEAR0 = 16
-ROOT0 = 41
+Y0 = 12
+NEAR0 = 17
+ROOT0 = 37
 X_TICK = 8
 AG_O, AG_T = (0, 0, 0, 0, 1, 1), (1, 0, 2, 3, 0, 1)
-RS_O, RS_T = (1, 0, 0, 0, 0), (0, 3, 2, 0, 1)
-B_O, B_T = (1, 1, 1, 0, 1, 0, 0, 0), (0, 1, 3, 3, 2, 2, 1, 0)
+RS_O, RS_T = (1, 0, 0, 0, 0), (0, 3, 0, 2, 1)
+B_O, B_T = (1, 1, 0, 1, 0, 1, 0, 0), (1, 0, 0, 3, 3, 2, 2, 1)
 A_O, A_T = (0, 0, 0, 0, 1, 1, 1, 1), (1, 0, 2, 3, 0, 2, 3, 1)
-Y_T = (3, 2, 1)
+Y_T = (3, 1, 2)
 QR = CH // 2
 AG_N = 2 * len(AG_T) * QR
+ROOT_N = 3 * QR
 A_TICK = (20, 21, 22, 23, 24, 25, 26, 27, 31, 35, 39, 43, 47, 48, 49, 51)
 F32 = jnp.float32
 BF16 = jnp.bfloat16
@@ -341,11 +342,15 @@
         return remote(out1.at[qx, :, cols], xbuf.at[:, cols], s_x.at[g], x_sem.at[g], xpart)
 
     def tick(step, carry):
-        n = step - ag_first
-
-        @pl.when((n >= 0) & (n < AG_N))
-        def _():
-            ag_step(n)
+        two = jnp.where((z == c) & (step >= ROOT_N), 1, 0)
+
+        @pl.loop(0, 1 + two)
+        def _(i):
+            n = jnp.where(two == 1, ROOT_N + (step - ROOT_N) * 2 + i, step - ag_first)
+
+            @pl.when((n >= 0) & (n < AG_N))
+            def _():
+                ag_step(n)
 
         m = step - rs_first
 

time: 250 us -> 245 us (0.980)
  Pallas kernels: 249 us -> 244 us
    pallas_call x1, Pallas kernels: 193 us -> 190 us  [panels(): pl.pallas_call(panels_kernel, out_shape=(jax.ShapeDtypeStruct((piece, wid...]
where the time goes in v6:
time: 245 us; the launch traced here: 244 us
  Pallas kernels  244 us (100%)
    pallas_call x1, Pallas kernels, panels(): pl.pallas_call(panels_kernel, out_shape=(jax.ShapeDtypeStruct((piece, wid...  190 us
    pallas_call x1, Pallas kernels, finish(): pl.pallas_call(finish_kernel, out_shape=(jax.ShapeDtypeStruct((rows, cols...  49.2 us
    pallas_call x1, Pallas kernels, hand_over(): pl.pallas_call(hand_over_kernel, out_shape=tuple((jax.ShapeDtypeStruct(a....  4.91 us

profile of v6, /device:TPU:0, one launch (start us, length us, event | category | flops | bytes accessed | tf_op | source)
XLA Modules:
  0.0 244.4 jit_solution(4863309812064553357)
XLA Ops:
  0.6 189.6 %panels.1 = (f32[512,512]{1,0:T(8,128)}, f32[512,512]{1,0:T(8,128)}, f32[512,512]{1,0:T(8,128)}, f32[512,512]{1,0:T(8,128)}) custom-call(f32[2048,4096]{1,0:T(8,128)} %trail.1, f32[512,512]{1,0:T(8,128)} %f1.1, f32[512,512]{1,0:T(8,128)} %inv1.3, f32[512,512]{1,0:T(8,128)} %f2.1, f32[512,512]{1,0:T(8,128)} %inv2.3, s32[1,96]{1,0:T(1,128)} %bitcast.2, ...), custom_call_target="tpu_custom_call" | custom-call | tf_op jit(solution)/shard_map/panels/pallas_call | solution.py:501
  190.3 49.2 %finish.1 = (f32[512,512]{1,0:T(8,128)}, f32[512,512]{1,0:T(8,128)}, f32[512,512]{1,0:T(8,128)}, f32[512,512]{1,0:T(8,128)}, f32[512,512]{1,0:T(8,128)}) custom-call(f32[512,512]{1,0:T(8,128)} %get-tuple-element.14.y1, f32[512,512]{1,0:T(8,128)} %get-tuple-element.15.y2t, f32[512,512]{1,0:T(8,128)} %get-tuple-element.16.n1, ...), custom_call_target="tpu_custom_call" | custom-call | tf_op jit(solution)/shard_map/finish/pallas_call | solution.py:673
  239.5 4.9 %hand_over.1 = (f32[512,512]{1,0:T(8,128)}, f32[512,512]{1,0:T(8,128)}, f32[512,512]{1,0:T(8,128)}, f32[512,512]{1,0:T(8,128)}, f32[512,512]{1,0:T(8,128)}) custom-call(f32[512,512]{1,0:T(8,128)} %get-tuple-element.18.refs_0_, f32[512,512]{1,0:T(8,128)} %get-tuple-element.19.refs_1_, f32[512,512]{1,0:T(8,128)} %get-tuple-element.20.refs_2_, ...), custom_call_target="tpu_custom_call" | custom-call | tf_op jit(solution)/shard_map/hand_over/pallas_call | solution.py:704
